TPU v7x, 1024 devices: a whole 4x8x16 slice. The times are simulated.
1024 devices in a mesh: dp: 16 (over y_hi, x, core), fsdp: 64 (over y_lo, z).
Axes of the slice: x: 4, y: 8 (y_hi: 2, y_lo: 4; y = y_hi * 4 + y_lo), z: 16, core: 2. Of those that a mesh axis runs over, the one named last changes fastest.
Arguments:
- inputs: bfloat16 [32768, 8192], P('dp', 'fsdp'), may hold values from -57 to 57
- out_grads: bfloat16 [32768, 28672], P('dp', 'fsdp'), may hold values from -57 to 57
- proj_in: bfloat16 [8192, 64], P('fsdp'), may hold values from -0.0625 to 0.0625
- proj_out: bfloat16 [28672, 64], P('fsdp'), may hold values from -0.03125 to 0.03125
- segment_ids: int32 [16, 2048], P('dp'), may hold values from 0 to 15, never falling along the last dimension, each value on 1 to 256 neighbouring positions
- sketch: float32 [4096, 512], P('fsdp'), may hold values from -0.09375 to 0.09375
Outputs:
- new_sketch: float32 [4096, 512], P('fsdp')
- precond: float32 [256, 512], P('dp')
Inputs may be any that keep to these rules, and one draw needn't show every extreme that they name: `segment_ids`: in each group the tokens, in order, form 16 examples of 1 to 256 tokens, and some example has exactly 256.
All inputs are finite; a program needn't handle non-finite values.
Results may differ from a plain program's by a relative error of at most 0.0003.
Values sent between devices are 32-bit elements; how exact they have to be, the bound alone decides.
No kernel may reach another device: no remote copies, remote signals or barrier semaphores. Data moves between devices by JAX's collectives and lax.ppermute only.
A program may use at most 32 MiB of HBM per device.

v0:
```python
import jax
import jax.numpy as jnp
from jax import lax
from jax.sharding import PartitionSpec as P

EX_GROUP = 16


rate_gain = 16.0
epsilon = 1e-06


def kron_features(onehot, left_part, right_part):
    tokens_here = onehot.shape[0]
    examples = onehot.shape[1]
    left_width = left_part.shape[1]
    weighted = (onehot[:, :, None] * left_part[:, None, :]).reshape(
        tokens_here, examples * left_width
    )
    summed = jnp.einsum("tm,tj->mj", weighted, right_part, precision=lax.Precision.HIGHEST)
    return summed.reshape(examples, left_width * right_part.shape[1])


def per_device(inputs, out_grads, proj_in, proj_out, segment_ids, sketch):
    high = lax.Precision.HIGHEST
    owners = lax.axis_size("fsdp")
    groups = lax.axis_size("dp")
    tokens_here = inputs.shape[0]
    proj_width = proj_in.shape[1]
    segment_row = segment_ids[0]
    onehot = (segment_row[:, None] == jnp.arange(EX_GROUP, dtype=jnp.int32)[None, :]).astype(
        jnp.float32
    )
    counts = jnp.sum(onehot, axis=0)
    own_rows = tokens_here // owners
    projected = lax.psum_scatter(
        jnp.concatenate(
            [
                jnp.dot(inputs, proj_in, preferred_element_type=jnp.float32),
                jnp.dot(out_grads, proj_out, preferred_element_type=jnp.float32),
            ],
            axis=1,
        ),
        "fsdp",
        scatter_dimension=0,
        tiled=True,
    )
    onehot_rows = lax.dynamic_slice_in_dim(onehot, lax.axis_index("fsdp") * own_rows, own_rows, 0)
    partial_features = kron_features(
        onehot_rows, projected[:, :proj_width], projected[:, proj_width:]
    )
    summed = lax.psum_scatter(partial_features, "fsdp", scatter_dimension=1, tiled=True)
    features = summed / counts[:, None]
    score_part = jnp.dot(features, sketch, precision=high)
    square_part = jnp.sum(features * features)
    scores, square_group = lax.psum((score_part, square_part), "fsdp")
    moment_part = jnp.dot(features.T, scores, precision=high)
    moment, total_sq = lax.psum((moment_part, square_group), "dp")
    step_rate = rate_gain / (total_sq + epsilon)
    fresh_sketch = sketch + step_rate * moment
    gram_part = jnp.dot(fresh_sketch.T, fresh_sketch, precision=high)
    gram_matrix = lax.psum(gram_part, "fsdp")
    lower_factor = jnp.linalg.cholesky(gram_matrix)
    new_basis = jax.scipy.linalg.solve_triangular(lower_factor, fresh_sketch.T, lower=True).T
    coefs = lax.psum(jnp.dot(features, new_basis, precision=high), "fsdp")
    spectrum_sum = lax.psum(jnp.sum(coefs * coefs, axis=0), "dp")
    spectrum_mean = spectrum_sum / (EX_GROUP * groups)
    precond = coefs / jnp.sqrt(spectrum_mean + epsilon)[None, :]
    return (new_basis, precond)


def solution(mesh):
    return jax.shard_map(
        per_device,
        mesh=mesh,
        in_specs=(
            P("dp", "fsdp"),
            P("dp", "fsdp"),
            P("fsdp", None),
            P("fsdp", None),
            P("dp", None),
            P("fsdp", None),
        ),
        out_specs=(P("fsdp", None), P("dp", None)),
        check_vma=False,
    )
```

profile of v0, /device:TPU:1, one launch (start us, length us, event | category | flops | bytes accessed | tf_op | source)
XLA Modules:
  0.0 2230.3 jit_solution(2386313322123385638)
XLA Ops:
  7.2 1.5 fusion.42
  8.7 0.1 copy-done
  8.8 1.3 fusion.43
  10.2 1.3 copy.26
  11.8 273.2 %reduce-scatter.7.cloned.1.call-done = f32[32,128]{1,0:T(8,128)} async-done(((f32[2048,128]{1,0:T(8,128)}), f32[32,128]{1,0:T(8,128)}) %reduce-scatter.7.cloned.1.call-update) | async-done | bytes 16400
  285.0 0.8 broadcast_multiply_fusion
  285.9 0.1 mul.36
  286.0 1.7 fusion.34
  287.7 0.2 reshape.55
  287.9 2.0 copy.28
  290.0 0.1 fusion.32
  290.1 306.4 %reduce-scatter.9.cloned.1.call-done = f32[64,16]{1,0:T(8,128)} async-done(((f32[4096,16]{1,0:T(8,128)}), f32[64,16]{1,0:T(8,128)}) %reduce-scatter.9.cloned.1.call-update) | async-done | bytes 4112
  596.5 0.8 copy.29
  597.3 0.7 multiply_reduce_fusion.1
  598.0 0.2 fusion.40
  598.2 242.2 %all-reduce.1 = (f32[16,512]{1,0:T(8,128)S(1)}, f32[]{:T(128)}) all-reduce(f32[16,512]{1,0:T(8,128)S(1)} %fusion.40, f32[]{:T(128)} %multiply_reduce_fusion.1), channel_id=1, replica_groups=mesh['dp'=16,'fsdp'=64] {'fsdp'}, use_global_device_ids=true, to_apply=%region_6.0 | all-reduce | flops 8193 | bytes 65544 | tf_op jit(solution)/shard_map/psum | solution.py:56
  840.4 1.0 fusion.39
  841.6 145.7 %psum.50 = f32[]{:T(128)} all-reduce(f32[]{:T(128)} %get-tuple-element.19), channel_id=1, replica_groups=mesh['dp'=16,'fsdp'=64] {'dp'}, use_global_device_ids=true, to_apply=%region_5.0 | all-reduce | flops 1 | bytes 8 | tf_op jit(solution)/shard_map/psum | solution.py:58
  987.9 135.8 %all-reduce.5.cloned.1.call-done = f32[64,512]{1,0:T(8,128)} async-done(((f32[64,512]{1,0:T(8,128)}), f32[64,512]{1,0:T(8,128)}) %all-reduce.5.cloned.1.call-update) | async-done | bytes 131088 | tf_op jit(solution)/shard_map/psum | solution.py:58
  1123.7 3.1 fusion.31
  1126.9 558.5 %all-reduce.7.cloned.1.call-done = f32[512,512]{0,1:T(8,128)} async-done(((f32[512,512]{0,1:T(8,128)}), f32[512,512]{0,1:T(8,128)}) %all-reduce.7.cloned.1.call-update) | async-done | bytes 1048592 | tf_op jit(solution)/shard_map/psum | solution.py:62
  1685.4 2.7 copy.23
  1688.1 1.4 fusion
  1689.5 1.0 copy-done.2
  1690.5 11.7 cholesky.104
  1702.3 0.1 cholesky.224
  1702.4 9.8 custom-call.31
  1712.2 1.2 constant_dynamic-update-slice_fusion.3
  1713.5 1.3 convolution_subtract_fusion
  1714.7 11.7 cholesky.217
  1726.5 9.9 custom-call.32
  1736.4 0.3 convolution_dynamic-update-slice_fusion
  1736.7 1.3 convolution_subtract_fusion.1
  1738.0 11.7 cholesky.238
  1749.8 0.7 compare_reduce_fusion.1
  1750.5 9.8 custom-call.33
  1760.3 0.2 convolution_dynamic-update-slice_fusion.1
  1760.5 1.2 convolution_subtract_fusion.2
  1761.7 12.0 cholesky.255
  1773.7 0.6 compare_reduce_fusion
  1774.4 0.7 compare_reduce_fusion.2
  1777.6 1.1 select_select_fusion
  1778.7 14.4 while.1
  1778.8 0.6 fusion.57
  1779.4 3.0 bitcast_dynamic-update-slice_fusion.2
  1782.4 0.6 fusion.57
  1783.0 3.0 bitcast_dynamic-update-slice_fusion.2
  1786.0 0.6 fusion.57
  1786.6 3.0 bitcast_dynamic-update-slice_fusion.2
  1789.6 0.6 fusion.57
  1790.2 2.9 bitcast_dynamic-update-slice_fusion.2
  1793.1 40.1 %custom-call.34 = f32[4,128,128]{1,2,0:T(8,128)S(1)} custom-call(f32[4,128,128]{2,1,0:T(8,128)} %get-tuple-element.9), custom_call_target="InvertDiagBlocksLowerTriangular" | custom-call | tf_op jit(solution)/shard_map/jit(_solve_triangular)/triangular_solve | solution.py:64
  1833.2 0.2 fusion.21
  1833.4 1.1 convolution_subtract_fusion.5
  1834.5 0.2 fusion.20
  1834.7 1.2 convolution_subtract_fusion.4
  1835.9 0.2 fusion.18
  1836.1 1.3 convolution_subtract_fusion.3
  1837.4 0.2 fusion.17
  1837.6 0.2 fusion.15
  1837.8 0.7 fusion.16
  1838.5 241.6 %psum.54 = f32[16,512]{1,0:T(8,128)S(1)} all-reduce(f32[16,512]{1,0:T(8,128)S(1)} %fusion.15), channel_id=1, replica_groups=mesh['dp'=16,'fsdp'=64] {'fsdp'}, use_global_device_ids=true, to_apply=%region_17.18 | all-reduce | flops 8192 | bytes 65536 | tf_op jit(solution)/shard_map/psum | solution.py:65
  2080.1 143.0 %psum.55 = f32[512]{0:T(512)S(1)} all-reduce(f32[512]{0:T(512)S(1)} %multiply_reduce_fusion), channel_id=1, replica_groups=mesh['dp'=16,'fsdp'=64] {'dp'}, use_global_device_ids=true, to_apply=%region_19.20 | all-reduce | flops 512 | bytes 4096 | tf_op jit(solution)/shard_map/psum | solution.py:66
  2223.1 0.6 broadcast_divide_fusion
  (39 shorter events, 1.0 us)
Async XLA Ops:
  7.2 1.7 copy-start
  7.2 277.8 %reduce-scatter.7.cloned.1.call-start = ((), (), s32[]{:S(2)}) async-start(), calls=%async_computation.4 | async-start | bytes 1064960
  10.2 1.4 copy-start.5
  11.6 584.9 %reduce-scatter.9.cloned.1.call-start = ((), (), s32[]{:S(2)}) async-start(), calls=%async_computation.5 | async-start | bytes 2129920
  287.9 310.1 %copy-start.3 = (f32[64,512]{1,0:T(8,128)S(1)}, f32[64,512]{1,0:T(8,128)}, u32[]{:S(2)}) copy-start(f32[64,512]{1,0:T(8,128)} %param.11) | copy-start | bytes 393220
  289.9 833.7 %all-reduce.5.cloned.1.call-start = ((), (), s32[]{:S(2)}) async-start(), calls=%async_computation.2 | async-start | bytes 262144 | tf_op jit(solution)/shard_map/psum | solution.py:58
  841.5 843.9 %all-reduce.7.cloned.1.call-start = ((), (), s32[]{:S(2)}) async-start(), calls=%async_computation.3 | async-start | bytes 2097152 | tf_op jit(solution)/shard_map/psum | solution.py:62
  1123.7 3.2 copy-start.4
  1685.4 2.7 copy-start.1
  1689.5 1.0 copy-start.2
Sparse Core Ops, SparseCore 0:
  11.7 273.2 reduce-scatter.6
  290.0 306.3 reduce-scatter.8
  841.6 281.9 all-reduce.4
  1127.4 557.9 all-reduce.6
where the time goes:
time: 2230 us
  waiting for transfers between devices  1270 us (57%)
  blocking collectives  773 us (35%)
  other arithmetic  125 us (6%)
  local copies, waits for them, and re-layouts  23 us (1%)
    unnamed x6, waiting for transfers between devices  580 us
    psum x1, waiting for transfers between devices, per_device(): gram_matrix = lax.psum(gram_part, 'fsdp')  559 us
    psum x1, blocking collectives, per_device(): scores, square_group = lax.psum((score_part, square_part), 'fsdp')  242 us
    psum x1, blocking collectives, per_device(): coefs = lax.psum(jnp.dot(features, new_basis, precision=high), 'fsdp')  242 us
    psum x1, blocking collectives, per_device(): moment, total_sq = lax.psum((moment_part, square_group), 'dp')  146 us
    psum x1, blocking collectives, per_device(): spectrum_sum = lax.psum(jnp.sum(coefs * coefs, axis=0), 'dp')  143 us
    psum x1, waiting for transfers between devices, per_device(): moment, total_sq = lax.psum((moment_part, square_group), 'dp')  136 us
    another operation x14, other arithmetic, per_device(): lower_factor = jnp.linalg.cholesky(gram_matrix)  78.8 us
  transfers between devices with their start and end apart: 4, of which 4 were waited for; matrix products, arithmetic and copies ran while one was open for 0% of the time, Pallas kernels for 0%

commit v1 on v0

v1 whole, which is shorter than its diff:
```python
import functools

import jax
import jax.numpy as jnp
from jax import lax
from jax.experimental import pallas as pl
from jax.experimental.pallas import tpu as pltpu
from jax.sharding import Mesh
from jax.sharding import PartitionSpec as P

HI = lax.Precision.HIGHEST
EX_GROUP = 16
DP = ("yh", "x", "c")
XC = ("x", "c")
FS = ("yl", "z")


def mm(a, b, dims, prec=HI):
    return lax.dot_general(a, b, (dims, ((), ())), precision=prec, preferred_element_type=jnp.float32)

def factor_block(d_ref, w_ref):
    nb = 128
    full = (8, nb)
    xs = [d_ref[8 * v: 8 * v + 8, :] for v in range(nb // 8)]
    ws = [w_ref[8 * v: 8 * v + 8, :] for v in range(nb // 8)]
    for p in range(nb // 8):
        base = 8 * p
        xr = [jnp.broadcast_to(xs[p][i:i + 1, :], full) for i in range(8)]
        wr = [jnp.broadcast_to(ws[p][i:i + 1, :], full) for i in range(8)]
        s = [[jnp.broadcast_to(xr[i][:, base + j:base + j + 1], full) for j in range(i + 1)] for i in range(8)]
        m = [[None] * 8 for _ in range(8)]
        inv = [None] * 8
        for k in range(8):
            inv[k] = 1.0 / s[k][k]
            for i in range(k + 1, 8):
                m[i][k] = s[i][k] * inv[k]
                for j in range(k + 1, i + 1):
                    s[i][j] = s[i][j] - m[i][k] * s[j][k]
        for i in range(8):
            for k in range(i):
                xr[i] = xr[i] - m[i][k] * xr[k]
                wr[i] = wr[i] - m[i][k] * wr[k]
        for i in range(8):
            w_ref[base + i: base + i + 1, :] = (wr[i] * lax.rsqrt(s[i][i]))[0:1, :]
        if p == nb // 8 - 1:
            break
        xv = [xr[i] * inv[i] for i in range(8)]
        wv = [wr[i] * inv[i] for i in range(8)]
        for i in range(7, -1, -1):
            for k in range(i + 1, 8):
                xv[i] = xv[i] - m[k][i] * xv[k]
                wv[i] = wv[i] - m[k][i] * wv[k]
        for q in range(p + 1, nb // 8):
            cols = [jnp.broadcast_to(xs[q][:, base + i:base + i + 1], full) for i in range(8)]
            for i in range(8):
                xs[q] = xs[q] - cols[i] * xv[i]
                ws[q] = ws[q] - cols[i] * wv[i]

def products_kernel(at_ref, tiles_ref, sketch_ref, gram_ref, sums_ref, features_ref):
    groups, half, lanes = tiles_ref.shape
    width = lanes // 2
    for g in range(groups):
        to = ((g % (groups // 2)) * 2 + g // (groups // 2)) * 2 * half
        tile = tiles_ref[g]
        features_ref[to:to + half, :] = tile[:, :width]
        features_ref[to + half:to + 2 * half, :] = tile[:, width:]
    rows = 4 * half
    features = features_ref[...]
    own = features_ref[pl.ds(pl.multiple_of(at_ref[0] * rows, rows), rows), :]
    inner = mm(own, features, ((1,), (1,)))
    scores = mm(own, sketch_ref[...], ((1,), (0,)))
    at = 0
    for part in (inner, scores, gram_ref[...]):
        for o in range(0, part.shape[1], lanes):
            sums_ref[at:at + part.shape[0], :] = part[:, o:o + lanes]
            at += part.shape[0]
    sums_ref[at:, :] = jnp.zeros((sums_ref.shape[0] - at, lanes), jnp.float32)


def products(block, tiles, sketch, gram_rows):
    vmem = pl.BlockSpec(memory_space=pltpu.VMEM)
    return pl.pallas_call(
        products_kernel,
        out_shape=(jax.ShapeDtypeStruct((512, 128), jnp.float32), jax.ShapeDtypeStruct((256, 64), jnp.float32)),
        in_specs=[pl.BlockSpec(memory_space=pltpu.SMEM), vmem, vmem, vmem],
        out_specs=(vmem, vmem),
        compiler_params=pltpu.CompilerParams(vmem_limit_bytes=24 * 1024 * 1024),
        name="products",
    )(block, tiles, sketch, gram_rows)


def finish_kernel(at_ref, sums_ref, f_ref, s_ref, ns_ref, co_ref, a_ref, x_ref, k_ref, p_ref, d_ref, w_ref):
    n = a_ref.shape[0]
    own, e = f_ref.shape[1], f_ref.shape[0]
    blocks = sums_ref.shape[0]
    rows, cut = e // blocks, n // blocks
    for b in range(blocks):
        at = 0
        for to, height in ((k_ref, rows), (p_ref, rows), (a_ref, cut)):
            for o in range(0, to.shape[1], 128):
                to[b * height:(b + 1) * height, o:o + 128] = sums_ref[b, at:at + height, :]
                at += height
    k = k_ref[...]
    p = p_ref[...]
    er = lax.broadcasted_iota(jnp.int32, (e, e), 0)
    ec = lax.broadcasted_iota(jnp.int32, (e, e), 1)
    total_sq = jnp.sum(jnp.sum(jnp.where(er == ec, k, 0.0), axis=0, keepdims=True), axis=1, keepdims=True)
    c = 16.0 / (total_sq + 1e-6)
    q = p + mm(k * c, p, ((1,), (0,)))
    x_ref[:own, :] = s_ref[...] + mm(f_ref[...] * c, p, ((0,), (0,)))
    x_ref[own:, :] = q
    a_ref[...] = a_ref[...] + mm(p * c, p + q, ((0,), (0,)))
    colid = lax.broadcasted_iota(jnp.int32, (128, n), 1)
    ri = lax.broadcasted_iota(jnp.int32, (128, 128), 0)
    ci = lax.broadcasted_iota(jnp.int32, (128, 128), 1)

    def step(b, carry):
        o = pl.multiple_of(b * 128, 128)
        d_ref[...] = a_ref[pl.ds(o, 128), pl.ds(o, 128)]
        w_ref[...] = jnp.where(ri == ci, 1.0, 0.0)
        factor_block(d_ref, w_ref)
        w = w_ref[...]
        r = mm(w, a_ref[pl.ds(o, 128), :], ((1,), (0,)))
        r = jnp.where(colid >= o + 128, r, 0.0)
        y = mm(x_ref[:, pl.ds(o, 128)], w, ((1,), (1,)))
        x_ref[...] = x_ref[...] - mm(y, r, ((1,), (0,)))
        x_ref[:, pl.ds(o, 128)] = y
        a_ref[...] = a_ref[...] - mm(r, r, ((0,), (0,)))
        return carry

    lax.fori_loop(0, n // 128, step, 0)
    ns_ref[...] = x_ref[:own, :]
    coefs = x_ref[own:, :]
    mean = jnp.sum(coefs * coefs, axis=0, keepdims=True) / e
    mine = x_ref[pl.ds(pl.multiple_of(own + at_ref[0] * EX_GROUP, EX_GROUP), EX_GROUP), :]
    co_ref[...] = mine / jnp.sqrt(mean + 1e-6)


def finish(at, sums, f, s):
    n, own, e = s.shape[1], s.shape[0], f.shape[0]
    vmem = pl.BlockSpec(memory_space=pltpu.VMEM)
    return pl.pallas_call(
        finish_kernel,
        out_shape=(jax.ShapeDtypeStruct((own, n), jnp.float32), jax.ShapeDtypeStruct((EX_GROUP, n), jnp.float32)),
        in_specs=[pl.BlockSpec(memory_space=pltpu.SMEM), vmem, vmem, vmem],
        out_specs=(vmem, vmem),
        scratch_shapes=[
            pltpu.VMEM((n, n), jnp.float32),
            pltpu.VMEM((own + e, n), jnp.float32),
            pltpu.VMEM((e, e), jnp.float32),
            pltpu.VMEM((e, n), jnp.float32),
            pltpu.VMEM((128, 128), jnp.float32),
            pltpu.VMEM((128, 128), jnp.float32),
        ],
        compiler_params=pltpu.CompilerParams(vmem_limit_bytes=40 * 1024 * 1024),
        name="finish",
    )(at, sums, f, s)


def exchange(x, axes):
    return lax.all_to_all(x, axes, 0, 0, tiled=True)


def spread(x, axes):
    return exchange(jnp.broadcast_to(x[None], (lax.axis_size(axes),) + x.shape), axes)


def outer_kernel(part_ref, seg_ref, out_ref):
    both = jnp.sum(part_ref[...], axis=0)
    tokens, width = both.shape[0], both.shape[1] // 2
    half = EX_GROUP // 2
    left = both[:, :width]
    col = lax.broadcasted_iota(jnp.int32, (width, width * half), 1)
    row = lax.broadcasted_iota(jnp.int32, (width, width * half), 0)
    repeat = jnp.where(col // half == row, 1.0, 0.0)
    wide = mm(left, repeat, ((1,), (0,)))
    slot = lax.broadcasted_iota(jnp.int32, (tokens, width * half), 1) % half
    seg = seg_ref[...]
    low = jnp.where(slot == seg, wide, 0.0)
    high = jnp.where(slot + half == seg, wide, 0.0)
    lane = lax.broadcasted_iota(jnp.int32, both.shape, 1)
    right = jnp.concatenate([both[:, width:], both[:, width:]], axis=1)
    right_low = jnp.where(lane < width, right, 0.0)
    right_high = jnp.where(lane < width, 0.0, right)
    out = mm(low, right_low, ((0,), (0,))) + mm(high, right_high, ((0,), (0,)))
    out_ref[...] = out.reshape(out_ref.shape)


def outer(parts, seg):
    width = parts.shape[2] // 2
    return pl.pallas_call(
        outer_kernel,
        out_shape=jax.ShapeDtypeStruct((width, EX_GROUP // 2, 2 * width), jnp.float32),
        in_specs=[pl.BlockSpec(memory_space=pltpu.VMEM)] * 2,
        out_specs=pl.BlockSpec(memory_space=pltpu.VMEM),
        compiler_params=pltpu.CompilerParams(vmem_limit_bytes=24 * 1024 * 1024),
        name="outer",
    )(parts, seg)


def per_device(inputs, out_grads, proj_in, proj_out, segment_ids, sketch):
    owners = lax.axis_size(FS)
    blocks = lax.axis_size(XC)
    tokens = inputs.shape[0]
    width = proj_in.shape[1]
    rank = sketch.shape[1]
    half = EX_GROUP // 2
    own_tokens = tokens // owners
    place = lax.axis_index(FS)
    block = lax.axis_index(XC)

    cut = rank // blocks
    gram_rows = mm(lax.dynamic_slice_in_dim(sketch, block * cut, cut, 1), sketch, ((0,), (0,)))

    segments = segment_ids[0]
    onehot = segments[:, None] == jnp.arange(EX_GROUP, dtype=jnp.int32)[None, :]
    counts = jnp.sum(onehot.astype(jnp.float32), axis=0)
    count_tile = jnp.repeat(counts.reshape(2, half).T, width, axis=1)
    own_segments = lax.dynamic_slice_in_dim(segments, place * own_tokens, own_tokens, 0)[:, None]

    projected = jnp.concatenate(
        [
            jnp.dot(inputs, proj_in, preferred_element_type=jnp.float32),
            jnp.dot(out_grads, proj_out, preferred_element_type=jnp.float32),
        ],
        axis=1,
    )
    parts = exchange(projected.reshape(owners, own_tokens, 2 * width), FS)
    partial_features = outer(parts, own_segments)
    tile = jnp.sum(exchange(partial_features, FS), axis=0) / count_tile
    tiles = spread(tile, DP)
    sums, features = products(block[None], tiles, sketch, gram_rows)
    chunk = jnp.sum(exchange(sums.reshape(owners, -1, 128), FS), axis=0)
    sums = spread(chunk, FS).reshape(sums.shape)[: 2 * EX_GROUP * 6 + cut * 4]
    sums = spread(sums, XC)
    at = block * 2 + lax.axis_index("yh")
    return finish(at[None], sums, features, sketch)


def solution(mesh):
    fine = Mesh(mesh.devices.reshape(2, 4, 2, 4, 16), ("yh", "x", "c", "yl", "z"))
    return jax.shard_map(
        per_device,
        mesh=fine,
        in_specs=(P(DP, FS), P(DP, FS), P(FS, None), P(FS, None), P(DP, None), P(FS, None)),
        out_specs=(P(FS, None), P(DP, None)),
        check_vma=False,
    )
```

time: 2230 us -> 254 us (0.11)
  waiting for transfers between devices: 1270 us -> 102 us
  blocking collectives: 773 us -> 51.5 us
  other arithmetic: 125 us -> 0.37 us
  starting transfers between devices: 0.16 us -> 51.4 us
  Pallas kernels: 0 us -> 40.2 us
    psum x4 -> x0, blocking collectives: 773 us -> none  [the longest x1 242 us: per_device(): scores, square_group = lax.psum((score_part, square_part), 'fsdp')]
    psum x2 -> x0, waiting for transfers between devices: 694 us -> none  [the longest x1 559 us: per_device(): gram_matrix = lax.psum(gram_part, 'fsdp')]
    unnamed x6 -> x0, waiting for transfers between devices: 580 us -> none
    another operation x17 -> x0, other arithmetic: 120 us -> none  [the longest x14 78.8 us: per_device(): lower_factor = jnp.linalg.cholesky(gram_matrix)]
    all_to_all x0 -> x4, waiting for transfers between devices: none -> 102 us  [exchange(): return lax.all_to_all(x, axes, 0, 0, tiled=True)]
    all_to_all x0 -> x2, blocking collectives: none -> 51.5 us  [exchange(): return lax.all_to_all(x, axes, 0, 0, tiled=True)]
    all_to_all x0 -> x4, starting transfers between devices: none -> 51.4 us  [exchange(): return lax.all_to_all(x, axes, 0, 0, tiled=True)]
    pallas_call x0 -> x3, Pallas kernels: none -> 40.2 us  [the longest x1 38.2 us: finish(): pl.pallas_call(finish_kernel, out_shape=(jax.ShapeDtypeStruct((own, n), j...]
where the time goes in v1:
time: 254 us; the launch traced here: 253 us
  waiting for transfers between devices  102 us (40%)
  blocking collectives  51.5 us (20%)
  starting transfers between devices  51.4 us (20%)
  Pallas kernels  40.2 us (16%)
  local copies, waits for them, and re-layouts  4.03 us (2%)
  matrix products  3.13 us (1%)
    all_to_all x4, waiting for transfers between devices, exchange(): return lax.all_to_all(x, axes, 0, 0, tiled=True)  102 us
    all_to_all x2, blocking collectives, exchange(): return lax.all_to_all(x, axes, 0, 0, tiled=True)  51.5 us
    all_to_all x4, starting transfers between devices, exchange(): return lax.all_to_all(x, axes, 0, 0, tiled=True)  51.4 us
    pallas_call x1, Pallas kernels, finish(): pl.pallas_call(finish_kernel, out_shape=(jax.ShapeDtypeStruct((own, n), j...  38.2 us
  transfers between devices with their start and end apart: 4, of which 4 were waited for; matrix products, arithmetic and copies ran while one was open for 0% of the time, Pallas kernels for 0%

profile of v1, /device:TPU:1, one launch (start us, length us, event | category | flops | bytes accessed | tf_op | source)
XLA Modules:
  0.0 252.9 jit_solution(15279135787561494738)
XLA Ops:
  0.6 0.0 copy-start
  0.6 1.5 fusion.3
  2.1 0.2 copy-done
  2.3 1.3 fusion.4
  3.6 0.1 pad_maximum_fusion
  3.7 0.0 copy-start.2
  3.7 1.3 copy.11
  5.0 0.0 copy-start.1
  5.0 23.5 %all-to-all-start = ((f32[64,32,128]{2,1,0:T(8,128)}), f32[64,32,128]{2,1,0:T(8,128)S(1)}, u32[]{:S(2)}, u32[]{:S(2)}) async-start(f32[64,32,128]{2,1,0:T(8,128)} %bitcast.16), calls=%async_computation | async-start | bytes 2097152 | tf_op jit(solution)/shard_map/all_to_all | solution.py:161
  28.5 0.0 copy-done.2
  28.5 0.1 dynamic-slice_bitcast_fusion
  28.6 0.1 copy.12.seg_ref
  28.7 50.4 %all-to-all-done.part_ref = f32[64,32,128]{2,1,0:T(8,128)S(1)} async-done(((f32[64,32,128]{2,1,0:T(8,128)}), f32[64,32,128]{2,1,0:T(8,128)S(1)}, u32[]{:S(2)}, u32[]{:S(2)}) %all-to-all-start) | async-done | bytes 1048608 | tf_op jit(solution)/shard_map/all_to_all | solution.py:161
  79.1 1.6 outer.1
  80.7 10.3 %all-to-all-start.1 = ((f32[64,8,128]{2,1,0:T(8,128)}), f32[64,8,128]{2,1,0:T(8,128)S(1)}, u32[]{:S(2)}, u32[]{:S(2)}) async-start(f32[64,8,128]{2,1,0:T(8,128)} %outer.1), calls=%async_computation.1 | async-start | bytes 524288 | tf_op jit(solution)/shard_map/all_to_all | solution.py:161
  91.0 0.1 convert_reduce_fusion
  91.1 0.1 reshape.32
  91.2 0.1 copy.13
  91.3 0.1 broadcast_in_dim.36
  91.3 0.1 reshape.33
  91.4 18.2 %all-to-all-done.1 = f32[64,8,128]{2,1,0:T(8,128)S(1)} async-done(((f32[64,8,128]{2,1,0:T(8,128)}), f32[64,8,128]{2,1,0:T(8,128)S(1)}, u32[]{:S(2)}, u32[]{:S(2)}) %all-to-all-start.1) | async-done | bytes 262176 | tf_op jit(solution)/shard_map/all_to_all | solution.py:161
  109.6 0.1 reduce_sum.27
  109.7 0.6 broadcast_in_dim.37
  110.3 10.2 %all-to-all-start.2 = ((f32[16,8,128]{2,1,0:T(8,128)}), f32[16,8,128]{2,1,0:T(8,128)S(1)}, u32[]{:S(2)}, u32[]{:S(2)}) async-start(f32[16,8,128]{2,1,0:T(8,128)} %broadcast_in_dim.37), calls=%async_computation.2 | async-start | bytes 131072 | tf_op jit(solution)/shard_map/all_to_all | solution.py:161
  120.5 0.0 copy-done.1
  120.5 0.4 fusion.gram_ref
  120.9 9.3 %all-to-all-done.2.tiles_ref = f32[16,8,128]{2,1,0:T(8,128)S(1)} async-done(((f32[16,8,128]{2,1,0:T(8,128)}), f32[16,8,128]{2,1,0:T(8,128)S(1)}, u32[]{:S(2)}, u32[]{:S(2)}) %all-to-all-start.2) | async-done | bytes 65568 | tf_op jit(solution)/shard_map/all_to_all | solution.py:161
  130.3 0.4 products.1
  130.6 25.1 %all_to_all.30 = f32[64,8,128]{2,1,0:T(8,128)S(1)} all-to-all(f32[64,8,128]{2,1,0:T(8,128)S(1)} %bitcast.15), channel_id=1, replica_groups=mesh['yh'=2,'x'=4,'c'=2,'yl'=4,'z'=16] {'yl','z'}, dimensions={0} | all-to-all | bytes 524288 | tf_op jit(solution)/shard_map/all_to_all | solution.py:161
  155.8 0.1 reduce_sum.29
  155.9 26.3 %all_to_all.31 = f32[64,8,128]{2,1,0:T(8,128)S(1)} all-to-all(f32[64,8,128]{2,1,0:T(8,128)S(1)} %broadcast_in_dim.38), channel_id=1, replica_groups=mesh['yh'=2,'x'=4,'c'=2,'yl'=4,'z'=16] {'yl','z'}, dimensions={0} | all-to-all | bytes 524288 | tf_op jit(solution)/shard_map/all_to_all | solution.py:161
  182.2 1.3 broadcast_in_dim.40
  183.6 7.5 %all-to-all-start.5 = ((f32[8,448,128]{2,1,0:T(8,128)}), f32[8,448,128]{2,1,0:T(8,128)}, u32[]{:S(2)}, u32[]{:S(2)}) async-start(f32[8,448,128]{2,1,0:T(8,128)} %broadcast_in_dim.40), calls=%async_computation.5 | async-start | bytes 3670016 | tf_op jit(solution)/shard_map/all_to_all | solution.py:161
  191.1 23.6 %all-to-all-done.5.sums_ref = f32[8,448,128]{2,1,0:T(8,128)} async-done(((f32[8,448,128]{2,1,0:T(8,128)}), f32[8,448,128]{2,1,0:T(8,128)}, u32[]{:S(2)}, u32[]{:S(2)}) %all-to-all-start.5) | async-done | bytes 1835040 | tf_op jit(solution)/shard_map/all_to_all | solution.py:161
  214.7 38.2 %finish.1 = (f32[64,512]{1,0:T(8,128)}, f32[16,512]{1,0:T(8,128)}) custom-call(s32[1]{0:T(128)} %bitcast.at_ref, f32[8,448,128]{2,1,0:T(8,128)} %all-to-all-done.5.sums_ref, f32[256,64]{1,0:T(8,128)S(1)} %get-tuple-element.5.f_ref, f32[64,512]{1,0:T(8,128)S(1)} %copy-done.1), custom_call_target="tpu_custom_call" | custom-call | tf_op jit(solution)/shard_map/finish/pallas_call | solution.py:142
  (3 shorter events, 0.0 us)
Async XLA Ops:
  0.6 1.7 copy-start
  3.7 24.8 %copy-start.2 = (s32[1,2048]{1,0:T(1,128)S(1)}, s32[1,2048]{1,0:T(1,128)}, u32[]{:S(2)}) copy-start(s32[1,2048]{1,0:T(1,128)} %param.10) | copy-start | bytes 24580
  5.0 115.5 %copy-start.1 = (f32[64,512]{1,0:T(8,128)S(1)}, f32[64,512]{1,0:T(8,128)}, u32[]{:S(2)}) copy-start(f32[64,512]{1,0:T(8,128)} %s_ref.1) | copy-start | bytes 393220
  5.0 74.1 %all-to-all-start = ((f32[64,32,128]{2,1,0:T(8,128)}), f32[64,32,128]{2,1,0:T(8,128)S(1)}, u32[]{:S(2)}, u32[]{:S(2)}) async-start(f32[64,32,128]{2,1,0:T(8,128)} %bitcast.16), calls=%async_computation | async-start | bytes 2097152 | tf_op jit(solution)/shard_map/all_to_all | solution.py:161
  80.7 28.9 %all-to-all-start.1 = ((f32[64,8,128]{2,1,0:T(8,128)}), f32[64,8,128]{2,1,0:T(8,128)S(1)}, u32[]{:S(2)}, u32[]{:S(2)}) async-start(f32[64,8,128]{2,1,0:T(8,128)} %outer.1), calls=%async_computation.1 | async-start | bytes 524288 | tf_op jit(solution)/shard_map/all_to_all | solution.py:161
  110.3 19.9 %all-to-all-start.2 = ((f32[16,8,128]{2,1,0:T(8,128)}), f32[16,8,128]{2,1,0:T(8,128)S(1)}, u32[]{:S(2)}, u32[]{:S(2)}) async-start(f32[16,8,128]{2,1,0:T(8,128)} %broadcast_in_dim.37), calls=%async_computation.2 | async-start | bytes 131072 | tf_op jit(solution)/shard_map/all_to_all | solution.py:161
  183.6 31.2 %all-to-all-start.5 = ((f32[8,448,128]{2,1,0:T(8,128)}), f32[8,448,128]{2,1,0:T(8,128)}, u32[]{:S(2)}, u32[]{:S(2)}) async-start(f32[8,448,128]{2,1,0:T(8,128)} %broadcast_in_dim.40), calls=%async_computation.5 | async-start | bytes 3670016 | tf_op jit(solution)/shard_map/all_to_all | solution.py:161

commit v2 on v1

--- a/solution.py
+++ b/solution.py
@@ -13,6 +13,7 @@
 DP = ("yh", "x", "c")
 XC = ("x", "c")
 FS = ("yl", "z")
+GRAM_HOPS = (("yl", 1), ("z", 1), ("yl", 2), ("z", 2), ("z", 4), ("z", 8))
 
 
 def mm(a, b, dims, prec=HI):
@@ -56,7 +57,7 @@
                 xs[q] = xs[q] - cols[i] * xv[i]
                 ws[q] = ws[q] - cols[i] * wv[i]
 
-def products_kernel(at_ref, tiles_ref, sketch_ref, gram_ref, sums_ref, features_ref):
+def products_kernel(at_ref, tiles_ref, sketch_ref, sums_ref, features_ref):
     groups, half, lanes = tiles_ref.shape
     width = lanes // 2
     for g in range(groups):
@@ -70,36 +71,41 @@
     inner = mm(own, features, ((1,), (1,)))
     scores = mm(own, sketch_ref[...], ((1,), (0,)))
     at = 0
-    for part in (inner, scores, gram_ref[...]):
+    for part in (inner, scores):
         for o in range(0, part.shape[1], lanes):
             sums_ref[at:at + part.shape[0], :] = part[:, o:o + lanes]
             at += part.shape[0]
     sums_ref[at:, :] = jnp.zeros((sums_ref.shape[0] - at, lanes), jnp.float32)
 
 
-def products(block, tiles, sketch, gram_rows):
+def products(block, tiles, sketch):
     vmem = pl.BlockSpec(memory_space=pltpu.VMEM)
     return pl.pallas_call(
         products_kernel,
-        out_shape=(jax.ShapeDtypeStruct((512, 128), jnp.float32), jax.ShapeDtypeStruct((256, 64), jnp.float32)),
-        in_specs=[pl.BlockSpec(memory_space=pltpu.SMEM), vmem, vmem, vmem],
+        out_shape=(jax.ShapeDtypeStruct((256, 128), jnp.float32), jax.ShapeDtypeStruct((256, 64), jnp.float32)),
+        in_specs=[pl.BlockSpec(memory_space=pltpu.SMEM), vmem, vmem],
         out_specs=(vmem, vmem),
         compiler_params=pltpu.CompilerParams(vmem_limit_bytes=24 * 1024 * 1024),
         name="products",
-    )(block, tiles, sketch, gram_rows)
-
-
-def finish_kernel(at_ref, sums_ref, f_ref, s_ref, ns_ref, co_ref, a_ref, x_ref, k_ref, p_ref, d_ref, w_ref):
+    )(block, tiles, sketch)
+
+
+def finish_kernel(at_ref, sums_ref, sums2_ref, gram_ref, gram2_ref, f_ref, s_ref, ns_ref, co_ref, a_ref, x_ref, k_ref, p_ref, d_ref, w_ref):
     n = a_ref.shape[0]
     own, e = f_ref.shape[1], f_ref.shape[0]
-    blocks = sums_ref.shape[0]
-    rows, cut = e // blocks, n // blocks
-    for b in range(blocks):
-        at = 0
-        for to, height in ((k_ref, rows), (p_ref, rows), (a_ref, cut)):
-            for o in range(0, to.shape[1], 128):
-                to[b * height:(b + 1) * height, o:o + 128] = sums_ref[b, at:at + height, :]
-                at += height
+    across = sums_ref.shape[0]
+    rows, cut = e // (2 * across), n // (2 * across)
+    for c in range(2):
+        core = at_ref[1] if c == 0 else 1 - at_ref[1]
+        sums, gram = (sums_ref, gram_ref) if c == 0 else (sums2_ref, gram2_ref)
+        for b in range(across):
+            at = 0
+            for to in (k_ref, p_ref):
+                for o in range(0, to.shape[1], 128):
+                    to[pl.ds(pl.multiple_of((2 * b + core) * rows, rows), rows), o:o + 128] = sums[b, at:at + rows, :]
+                    at += rows
+            there = lax.rem(at_ref[2] + across - b, across)
+            a_ref[pl.ds(pl.multiple_of((2 * there + core) * cut, cut), cut), :] = gram[b]
     k = k_ref[...]
     p = p_ref[...]
     er = lax.broadcasted_iota(jnp.int32, (e, e), 0)
@@ -136,13 +142,13 @@
     co_ref[...] = mine / jnp.sqrt(mean + 1e-6)
 
 
-def finish(at, sums, f, s):
+def finish(at, sums, sums2, gram, gram2, f, s):
     n, own, e = s.shape[1], s.shape[0], f.shape[0]
     vmem = pl.BlockSpec(memory_space=pltpu.VMEM)
     return pl.pallas_call(
         finish_kernel,
         out_shape=(jax.ShapeDtypeStruct((own, n), jnp.float32), jax.ShapeDtypeStruct((EX_GROUP, n), jnp.float32)),
-        in_specs=[pl.BlockSpec(memory_space=pltpu.SMEM), vmem, vmem, vmem],
+        in_specs=[pl.BlockSpec(memory_space=pltpu.SMEM)] + [vmem] * 6,
         out_specs=(vmem, vmem),
         scratch_shapes=[
             pltpu.VMEM((n, n), jnp.float32),
@@ -154,7 +160,7 @@
         ],
         compiler_params=pltpu.CompilerParams(vmem_limit_bytes=40 * 1024 * 1024),
         name="finish",
-    )(at, sums, f, s)
+    )(at, sums, sums2, gram, gram2, f, s)
 
 
 def exchange(x, axes):
@@ -163,6 +169,10 @@
 
 def spread(x, axes):
     return exchange(jnp.broadcast_to(x[None], (lax.axis_size(axes),) + x.shape), axes)
+
+
+def swap(x, axis, bit):
+    return lax.ppermute(x, axis, [(i, i ^ bit) for i in range(lax.axis_size(axis))])
 
 
 def outer_kernel(part_ref, seg_ref, out_ref):
@@ -209,9 +219,6 @@
     place = lax.axis_index(FS)
     block = lax.axis_index(XC)
 
-    cut = rank // blocks
-    gram_rows = mm(lax.dynamic_slice_in_dim(sketch, block * cut, cut, 1), sketch, ((0,), (0,)))
-
     segments = segment_ids[0]
     onehot = segments[:, None] == jnp.arange(EX_GROUP, dtype=jnp.int32)[None, :]
     counts = jnp.sum(onehot.astype(jnp.float32), axis=0)
@@ -225,16 +232,37 @@
         ],
         axis=1,
     )
-    parts = exchange(projected.reshape(owners, own_tokens, 2 * width), FS)
-    partial_features = outer(parts, own_segments)
-    tile = jnp.sum(exchange(partial_features, FS), axis=0) / count_tile
+    cut = rank // blocks
+    sketch_cols = lax.dynamic_slice_in_dim(sketch, block * cut, cut, 1)
+    sketch_cols, projected = lax.optimization_barrier((sketch_cols, projected))
+    gram = mm(sketch_cols, sketch, ((0,), (0,)))
+    for axis, bit in GRAM_HOPS[:3]:
+        gram = gram + swap(gram, axis, bit)
+    parts = exchange(projected.reshape(4, -1, 2 * width), "yl")
+    parts, gram = lax.optimization_barrier((parts, gram))
+    for axis, bit in GRAM_HOPS[3:5]:
+        gram = gram + swap(gram, axis, bit)
+    parts = exchange(jnp.sum(parts, axis=0).reshape(-1, own_tokens, 2 * width), "z")
+    parts, gram = lax.optimization_barrier((parts, gram))
+    for axis, bit in GRAM_HOPS[5:]:
+        gram = gram + swap(gram, axis, bit)
+    partial_features = exchange(outer(parts, own_segments), FS)
+    partial_features, gram = lax.optimization_barrier((partial_features, gram))
+    tile = jnp.sum(partial_features, axis=0) / count_tile
     tiles = spread(tile, DP)
-    sums, features = products(block[None], tiles, sketch, gram_rows)
-    chunk = jnp.sum(exchange(sums.reshape(owners, -1, 128), FS), axis=0)
-    sums = spread(chunk, FS).reshape(sums.shape)[: 2 * EX_GROUP * 6 + cut * 4]
-    sums = spread(sums, XC)
-    at = block * 2 + lax.axis_index("yh")
-    return finish(at[None], sums, features, sketch)
+    features_sums = products(block[None], tiles, sketch)
+    sums, features = features_sums
+    around = lax.axis_size("x")
+    gram = jnp.stack([gram] + [lax.ppermute(gram, "x", [(i, (i + s) % around) for i in range(around)]) for s in range(1, around)])
+    sums = exchange(sums.reshape(owners, -1, 128), FS)
+    sums, gram = lax.optimization_barrier((sums, gram))
+    other_gram = swap(gram, "c", 1)
+    sums = spread(jnp.sum(sums, axis=0), FS)
+    sums, other_gram = lax.optimization_barrier((sums, other_gram))
+    sums = spread(sums.reshape(-1, 128)[: 2 * EX_GROUP * 6], "x")
+    other_sums = swap(sums, "c", 1)
+    at = jnp.stack([block * 2 + lax.axis_index("yh"), lax.axis_index("c"), lax.axis_index("x")])
+    return finish(at, sums, other_sums, gram, other_gram, features, sketch)
 
 
 def solution(mesh):

time: 254 us -> 277 us (1.091)
  starting transfers between devices: 51.4 us -> 103 us
  waiting for transfers between devices: 102 us -> 66.4 us
  blocking collectives: 51.5 us -> 57.8 us
    all_to_all x4, waiting for transfers between devices: 102 us -> 1.07 us  [exchange(): return lax.all_to_all(x, axes, 0, 0, tiled=True)]
    ppermute x0 -> x11, waiting for transfers between devices: none -> 65.3 us  [the longest x8 59.9 us: swap(): lax.ppermute(x, axis, [(i, i ^ bit) for i in range(lax.axis_size(axis))])]
    ppermute x0 -> x11, starting transfers between devices: none -> 61 us  [the longest x8 53.2 us: swap(): lax.ppermute(x, axis, [(i, i ^ bit) for i in range(lax.axis_size(axis))])]
    all_to_all x4, starting transfers between devices: 51.4 us -> 42.2 us  [exchange(): return lax.all_to_all(x, axes, 0, 0, tiled=True)]
    all_to_all x2 -> x3, blocking collectives: 51.5 us -> 57.8 us  [exchange(): return lax.all_to_all(x, axes, 0, 0, tiled=True)]
  transfers between devices with their start and end apart: 4 -> 15, of which waited for: 4 -> 10; matrix products, arithmetic and copies ran while one was open for 0% -> 0% of each run, Pallas kernels for 0% -> 0%
where the time goes in v2:
time: 277 us; the launch traced here: 276 us
  starting transfers between devices  103 us (37%)
  waiting for transfers between devices  66.4 us (24%)
  blocking collectives  57.8 us (21%)
  Pallas kernels  40.4 us (15%)
  local copies, waits for them, and re-layouts  3.98 us (1%)
    ppermute x8, waiting for transfers between devices, swap(): lax.ppermute(x, axis, [(i, i ^ bit) for i in range(lax.axis_size(axis))])  59.9 us
    all_to_all x3, blocking collectives, exchange(): return lax.all_to_all(x, axes, 0, 0, tiled=True)  57.8 us
    ppermute x8, starting transfers between devices, swap(): lax.ppermute(x, axis, [(i, i ^ bit) for i in range(lax.axis_size(axis))])  53.2 us
    all_to_all x4, starting transfers between devices, exchange(): return lax.all_to_all(x, axes, 0, 0, tiled=True)  42.2 us
    pallas_call x1, Pallas kernels, finish(): pl.pallas_call(finish_kernel, out_shape=(jax.ShapeDtypeStruct((own, n), j...  37.7 us
    ppermute x3, starting transfers between devices, per_device(): lax.ppermute(gram, 'x', [(i, (i + s) % around) for i in range(around)])  7.81 us
  transfers between devices with their start and end apart: 15, of which 10 were waited for; matrix products, arithmetic and copies ran while one was open for 0% of the time, Pallas kernels for 0%

profile of v2, /device:TPU:1, one launch (start us, length us, event | category | flops | bytes accessed | tf_op | source)
XLA Modules:
  0.0 276.4 jit_solution(10627597558216010594)
XLA Ops:
  0.6 0.0 copy-start
  0.6 0.0 copy-start.2
  0.7 0.0 copy-start.3
  0.7 1.0 constant_dynamic-slice_fusion
  1.7 0.5 copy-done
  2.2 1.3 fusion.2
  3.4 0.0 copy-done.2
  3.4 0.0 copy-done.3
  3.4 0.3 fusion
  3.7 0.1 pad_maximum_fusion
  3.8 0.0 copy-start.1
  3.9 1.1 copy.23
  4.9 5.4 %all-to-all-start = ((f32[4,512,128]{1,2,0:T(8,128)}), f32[4,512,128]{1,2,0:T(8,128)}, u32[]{:S(2)}, u32[]{:S(2)}) async-start(f32[4,512,128]{1,2,0:T(8,128)} %bitcast.24), calls=%async_computation | async-start | bytes 2097152 | tf_op jit(solution)/shard_map/all_to_all | solution.py:167
  10.4 0.0 copy-done.1
  10.4 0.3 fusion.1
  10.7 3.4 %collective-permute-start = (f32[64,512]{1,0:T(8,128)S(1)}, f32[64,512]{1,0:T(8,128)S(1)}, u32[]{:S(2)}, u32[]{:S(2)}) collective-permute-start(f32[64,512]{1,0:T(8,128)S(1)} %fusion.1), channel_id=1, source_target_pairs={{0,16},{16,0},{32,48},{48,32},{1,17},{17,1},{33,49},{49,33},{2,18}... | collective-permute-start | bytes 393224 | tf_op jit(solution)/shard_map/ppermute | solution.py:175
  14.1 7.0 %collective-permute-done = f32[64,512]{1,0:T(8,128)S(1)} collective-permute-done((f32[64,512]{1,0:T(8,128)S(1)}, f32[64,512]{1,0:T(8,128)S(1)}, u32[]{:S(2)}, u32[]{:S(2)}) %collective-permute-start) | collective-permute-done | bytes 131104 | tf_op jit(solution)/shard_map/ppermute | solution.py:175
  21.1 0.0 copy-start.4
  21.1 12.6 %collective-permute-start.1 = (f32[64,512]{1,0:T(8,128)S(1)}, f32[64,512]{1,0:T(8,128)S(1)}, u32[]{:S(2)}, u32[]{:S(2)}) collective-permute-start(f32[64,512]{1,0:T(8,128)S(1)} %add.36), channel_id=1, source_target_pairs={{0,1},{1,0},{2,3},{3,2},{4,5},{5,4},{6,7},{7,6},{8,9},{9,8},{10,11... | collective-permute-start | bytes 393224 | tf_op jit(solution)/shard_map/ppermute | solution.py:175
  33.7 2.7 collective-permute-done.1
  36.5 5.3 %collective-permute-start.2 = (f32[64,512]{1,0:T(8,128)S(1)}, f32[64,512]{1,0:T(8,128)S(1)}, u32[]{:S(2)}, u32[]{:S(2)}) collective-permute-start(f32[64,512]{1,0:T(8,128)S(1)} %add.37), channel_id=1, source_target_pairs={{0,32},{16,48},{32,0},{48,16},{1,33},{17,49},{33,1},{49,17},{2,34}... | collective-permute-start | bytes 393224 | tf_op jit(solution)/shard_map/ppermute | solution.py:175
  41.7 3.7 %collective-permute-done.2 = f32[64,512]{1,0:T(8,128)S(1)} collective-permute-done((f32[64,512]{1,0:T(8,128)S(1)}, f32[64,512]{1,0:T(8,128)S(1)}, u32[]{:S(2)}, u32[]{:S(2)}) %collective-permute-start.2) | collective-permute-done | bytes 131104 | tf_op jit(solution)/shard_map/ppermute | solution.py:175
  45.5 0.0 all-to-all-done
  45.5 1.3 reduce_sum.36
  46.8 0.8 copy.17
  47.7 17.9 %all-to-all-start.1 = ((f32[16,32,128]{2,1,0:T(8,128)}), f32[16,32,128]{2,1,0:T(8,128)S(1)}, u32[]{:S(2)}, u32[]{:S(2)}) async-start(f32[16,32,128]{2,1,0:T(8,128)} %bitcast.4), calls=%async_computation.1 | async-start | bytes 524288 | tf_op jit(solution)/shard_map/all_to_all | solution.py:167
  65.6 4.2 %collective-permute-start.3 = (f32[64,512]{1,0:T(8,128)S(1)}, f32[64,512]{1,0:T(8,128)S(1)}, u32[]{:S(2)}, u32[]{:S(2)}) collective-permute-start(f32[64,512]{1,0:T(8,128)S(1)} %add.38), channel_id=1, source_target_pairs={{0,2},{1,3},{2,0},{3,1},{4,6},{5,7},{6,4},{7,5},{8,10},{9,11},{10,... | collective-permute-start | bytes 393224 | tf_op jit(solution)/shard_map/ppermute | solution.py:175
  69.8 12.7 %collective-permute-done.3 = f32[64,512]{1,0:T(8,128)S(1)} collective-permute-done((f32[64,512]{1,0:T(8,128)S(1)}, f32[64,512]{1,0:T(8,128)S(1)}, u32[]{:S(2)}, u32[]{:S(2)}) %collective-permute-start.3) | collective-permute-done | bytes 131104 | tf_op jit(solution)/shard_map/ppermute | solution.py:175
  82.5 7.1 %collective-permute-start.4 = (f32[64,512]{1,0:T(8,128)S(1)}, f32[64,512]{1,0:T(8,128)S(1)}, u32[]{:S(2)}, u32[]{:S(2)}) collective-permute-start(f32[64,512]{1,0:T(8,128)S(1)} %add.39), channel_id=1, source_target_pairs={{0,4},{1,5},{2,6},{3,7},{4,0},{5,1},{6,2},{7,3},{8,12},{9,13},{10,... | collective-permute-start | bytes 393224 | tf_op jit(solution)/shard_map/ppermute | solution.py:175
  89.7 0.0 copy-done.4
  89.7 0.1 dynamic-slice_bitcast_fusion
  89.8 0.1 copy.18.seg_ref
  89.8 11.8 %collective-permute-done.4 = f32[64,512]{1,0:T(8,128)S(1)} collective-permute-done((f32[64,512]{1,0:T(8,128)S(1)}, f32[64,512]{1,0:T(8,128)S(1)}, u32[]{:S(2)}, u32[]{:S(2)}) %collective-permute-start.4) | collective-permute-done | bytes 131104 | tf_op jit(solution)/shard_map/ppermute | solution.py:175
  101.6 0.0 all-to-all-done.1.part_ref
  101.6 1.6 outer.1
  103.2 11.8 %all-to-all-start.2 = ((f32[64,8,128]{2,1,0:T(8,128)}), f32[64,8,128]{2,1,0:T(8,128)S(1)}, u32[]{:S(2)}, u32[]{:S(2)}) async-start(f32[64,8,128]{2,1,0:T(8,128)} %outer.1), calls=%async_computation.2 | async-start | bytes 524288 | tf_op jit(solution)/shard_map/all_to_all | solution.py:167
  115.0 11.6 %collective-permute-start.5 = (f32[64,512]{1,0:T(8,128)S(1)}, f32[64,512]{1,0:T(8,128)S(1)}, u32[]{:S(2)}, u32[]{:S(2)}) collective-permute-start(f32[64,512]{1,0:T(8,128)S(1)} %add.40), channel_id=1, source_target_pairs={{0,8},{1,9},{2,10},{3,11},{4,12},{5,13},{6,14},{7,15},{8,0},{9,1},... | collective-permute-start | bytes 393224 | tf_op jit(solution)/shard_map/ppermute | solution.py:175
  126.6 0.1 convert_reduce_fusion
  126.7 0.1 reshape.36
  126.8 0.1 copy.19
  126.9 0.1 broadcast_in_dim.32
  127.0 0.1 reshape.37
  127.1 20.8 %collective-permute-done.5 = f32[64,512]{1,0:T(8,128)S(1)} collective-permute-done((f32[64,512]{1,0:T(8,128)S(1)}, f32[64,512]{1,0:T(8,128)S(1)}, u32[]{:S(2)}, u32[]{:S(2)}) %collective-permute-start.5) | collective-permute-done | bytes 131104 | tf_op jit(solution)/shard_map/ppermute | solution.py:175
  147.9 0.0 all-to-all-done.2
  147.9 0.1 reduce_sum.37
  148.0 20.5 %all_to_all.35.tiles_ref = f32[16,8,128]{2,1,0:T(8,128)S(1)} all-to-all(f32[16,8,128]{2,1,0:T(8,128)S(1)} %broadcast_in_dim.33), channel_id=1, replica_groups=mesh['yh'=2,'x'=4,'c'=2,'yl'=4,'z'=16] {'yh','x','c'}, dimensions={0} | all-to-all | bytes 131072 | tf_op jit(solution)/shard_map/all_to_all | solution.py:167
  168.5 1.0 products.1
  169.5 7.1 %all-to-all-start.4 = ((f32[64,4,128]{2,1,0:T(4,128)}), f32[64,4,128]{2,1,0:T(4,128)S(1)}, u32[]{:S(2)}, u32[]{:S(2)}) async-start(f32[64,4,128]{2,1,0:T(4,128)} %bitcast.8), calls=%async_computation.4 | async-start | bytes 262144 | tf_op jit(solution)/shard_map/all_to_all | solution.py:167
  176.6 2.9 %collective-permute-start.8 = (f32[64,512]{1,0:T(8,128)S(1)}, f32[64,512]{1,0:T(8,128)S(1)}, u32[]{:S(2)}, u32[]{:S(2)}) collective-permute-start(f32[64,512]{1,0:T(8,128)S(1)} %add.43), channel_id=1, source_target_pairs={{0,384},{128,0},{256,128},{384,256},{1,385},{129,1},{257,129},{385... | collective-permute-start | bytes 393224 | tf_op jit(solution)/shard_map/ppermute | solution.py:256
  179.5 3.0 %collective-permute-start.7 = (f32[64,512]{1,0:T(8,128)S(1)}, f32[64,512]{1,0:T(8,128)S(1)}, u32[]{:S(2)}, u32[]{:S(2)}) collective-permute-start(f32[64,512]{1,0:T(8,128)S(1)} %add.43), channel_id=1, source_target_pairs={{0,256},{128,384},{256,0},{384,128},{1,257},{129,385},{257,1},{385... | collective-permute-start | bytes 393224 | tf_op jit(solution)/shard_map/ppermute | solution.py:256
  182.5 1.9 collective-permute-start.6
  184.4 0.0 collective-permute-done.8
  184.4 2.6 collective-permute-done.7
  187.0 2.8 %collective-permute-done.6 = f32[64,512]{1,0:T(8,128)S(1)} collective-permute-done((f32[64,512]{1,0:T(8,128)S(1)}, f32[64,512]{1,0:T(8,128)S(1)}, u32[]{:S(2)}, u32[]{:S(2)}) %collective-permute-start.6) | collective-permute-done | bytes 131104 | tf_op jit(solution)/shard_map/ppermute | solution.py:256
  189.9 1.1 all-to-all-done.4
  191.0 4.1 %collective-permute-start.9 = (f32[4,64,512]{2,1,0:T(8,128)S(1)}, f32[4,64,512]{2,1,0:T(8,128)S(1)}, u32[]{:S(2)}, u32[]{:S(2)}) collective-permute-start(f32[4,64,512]{2,1,0:T(8,128)S(1)} %pad_maximum_fusion.1.gram_ref), channel_id=1, source_target_pairs={{0,64},{64,0},{1,65},{65,1},{2,66},{66,2},{3,67},{67,3},{4,68},{68... | collective-permute-start | bytes 1572872 | tf_op jit(solution)/shard_map/ppermute | solution.py:175
  195.1 0.1 reduce_sum.39
  195.2 28.7 %all_to_all.36 = f32[64,4,128]{2,1,0:T(4,128)S(1)} all-to-all(f32[64,4,128]{2,1,0:T(4,128)S(1)} %broadcast_in_dim.34), channel_id=1, replica_groups=mesh['yh'=2,'x'=4,'c'=2,'yl'=4,'z'=16] {'yl','z'}, dimensions={0} | all-to-all | bytes 262144 | tf_op jit(solution)/shard_map/all_to_all | solution.py:167
  223.8 0.0 collective-permute-done.9.gram2_ref
  223.9 8.7 %all_to_all.37.sums_ref = f32[4,192,128]{2,1,0:T(8,128)S(1)} all-to-all(f32[4,192,128]{2,1,0:T(8,128)S(1)} %broadcast_in_dim.36), channel_id=1, replica_groups=mesh['yh'=2,'x'=4,'c'=2,'yl'=4,'z'=16] {'x'}, dimensions={0} | all-to-all | bytes 786432 | tf_op jit(solution)/shard_map/all_to_all | solution.py:167
  232.5 4.9 %collective-permute-start.10 = (f32[4,192,128]{2,1,0:T(8,128)S(1)}, f32[4,192,128]{2,1,0:T(8,128)}, u32[]{:S(2)}, u32[]{:S(2)}) collective-permute-start(f32[4,192,128]{2,1,0:T(8,128)S(1)} %all_to_all.37.sums_ref), channel_id=1, source_target_pairs={{0,64},{64,0},{1,65},{65,1},{2,66},{66,2},{3,67},{67,3},{4,68},{68... | collective-permute-start | bytes 1179656 | tf_op jit(solution)/shard_map/ppermute | solution.py:175
  237.4 0.1 pad_add_fusion.at_ref
  237.5 1.2 collective-permute-done.10.sums2_ref
  238.7 37.7 %finish.1 = (f32[64,512]{1,0:T(8,128)}, f32[16,512]{1,0:T(8,128)}) custom-call(s32[3]{0:T(128)S(1)} %pad_add_fusion.at_ref, f32[4,192,128]{2,1,0:T(8,128)S(1)} %all_to_all.37.sums_ref, f32[4,192,128]{2,1,0:T(8,128)} %collective-permute-done.10.sums2_ref, f32[4,64,512]{2,1,0:T(8,128)S(1)} %pad_maximum_fusion.1.gram_ref, ...), custom_call_target="tpu_custom_call" | custom-call | tf_op jit(solution)/shard_map/finish/pallas_call | solution.py:148
  (12 shorter events, 0.2 us)
Async XLA Ops:
  0.6 1.5 copy-start
  0.6 2.8 %copy-start.2 = (bf16[2048,128]{1,0:T(8,128)(2,1)S(1)}, bf16[2048,128]{1,0:T(8,128)(2,1)}, u32[]{:S(2)}) copy-start(bf16[2048,128]{1,0:T(8,128)(2,1)} %param.6) | copy-start | bytes 1572868
  0.7 2.8 %copy-start.3 = (bf16[128,64]{0,1:T(8,128)(2,1)S(1)}, bf16[128,64]{0,1:T(8,128)(2,1)}, u32[]{:S(2)}) copy-start(bf16[128,64]{0,1:T(8,128)(2,1)} %param.8) | copy-start | bytes 49156
  3.8 6.5 %copy-start.1 = (f32[64,512]{1,0:T(8,128)S(1)}, f32[64,512]{1,0:T(8,128)}, u32[]{:S(2)}) copy-start(f32[64,512]{1,0:T(8,128)} %s_ref.1) | copy-start | bytes 393220
  4.9 40.6 %all-to-all-start = ((f32[4,512,128]{1,2,0:T(8,128)}), f32[4,512,128]{1,2,0:T(8,128)}, u32[]{:S(2)}, u32[]{:S(2)}) async-start(f32[4,512,128]{1,2,0:T(8,128)} %bitcast.24), calls=%async_computation | async-start | bytes 2097152 | tf_op jit(solution)/shard_map/all_to_all | solution.py:167
  10.7 10.4 %collective-permute-start = (f32[64,512]{1,0:T(8,128)S(1)}, f32[64,512]{1,0:T(8,128)S(1)}, u32[]{:S(2)}, u32[]{:S(2)}) collective-permute-start(f32[64,512]{1,0:T(8,128)S(1)} %fusion.1), channel_id=1, source_target_pairs={{0,16},{16,0},{32,48},{48,32},{1,17},{17,1},{33,49},{49,33},{2,18}... | collective-permute-start | bytes 393224 | tf_op jit(solution)/shard_map/ppermute | solution.py:175
  21.1 68.6 %copy-start.4 = (s32[1,2048]{1,0:T(1,128)S(1)}, s32[1,2048]{1,0:T(1,128)}, u32[]{:S(2)}) copy-start(s32[1,2048]{1,0:T(1,128)} %param.10) | copy-start | bytes 24580
  21.1 15.4 %collective-permute-start.1 = (f32[64,512]{1,0:T(8,128)S(1)}, f32[64,512]{1,0:T(8,128)S(1)}, u32[]{:S(2)}, u32[]{:S(2)}) collective-permute-start(f32[64,512]{1,0:T(8,128)S(1)} %add.36), channel_id=1, source_target_pairs={{0,1},{1,0},{2,3},{3,2},{4,5},{5,4},{6,7},{7,6},{8,9},{9,8},{10,11... | collective-permute-start | bytes 393224 | tf_op jit(solution)/shard_map/ppermute | solution.py:175
  36.5 9.0 %collective-permute-start.2 = (f32[64,512]{1,0:T(8,128)S(1)}, f32[64,512]{1,0:T(8,128)S(1)}, u32[]{:S(2)}, u32[]{:S(2)}) collective-permute-start(f32[64,512]{1,0:T(8,128)S(1)} %add.37), channel_id=1, source_target_pairs={{0,32},{16,48},{32,0},{48,16},{1,33},{17,49},{33,1},{49,17},{2,34}... | collective-permute-start | bytes 393224 | tf_op jit(solution)/shard_map/ppermute | solution.py:175
  47.7 54.0 %all-to-all-start.1 = ((f32[16,32,128]{2,1,0:T(8,128)}), f32[16,32,128]{2,1,0:T(8,128)S(1)}, u32[]{:S(2)}, u32[]{:S(2)}) async-start(f32[16,32,128]{2,1,0:T(8,128)} %bitcast.4), calls=%async_computation.1 | async-start | bytes 524288 | tf_op jit(solution)/shard_map/all_to_all | solution.py:167
  65.6 16.9 %collective-permute-start.3 = (f32[64,512]{1,0:T(8,128)S(1)}, f32[64,512]{1,0:T(8,128)S(1)}, u32[]{:S(2)}, u32[]{:S(2)}) collective-permute-start(f32[64,512]{1,0:T(8,128)S(1)} %add.38), channel_id=1, source_target_pairs={{0,2},{1,3},{2,0},{3,1},{4,6},{5,7},{6,4},{7,5},{8,10},{9,11},{10,... | collective-permute-start | bytes 393224 | tf_op jit(solution)/shard_map/ppermute | solution.py:175
  82.5 19.1 %collective-permute-start.4 = (f32[64,512]{1,0:T(8,128)S(1)}, f32[64,512]{1,0:T(8,128)S(1)}, u32[]{:S(2)}, u32[]{:S(2)}) collective-permute-start(f32[64,512]{1,0:T(8,128)S(1)} %add.39), channel_id=1, source_target_pairs={{0,4},{1,5},{2,6},{3,7},{4,0},{5,1},{6,2},{7,3},{8,12},{9,13},{10,... | collective-permute-start | bytes 393224 | tf_op jit(solution)/shard_map/ppermute | solution.py:175
  103.2 44.7 %all-to-all-start.2 = ((f32[64,8,128]{2,1,0:T(8,128)}), f32[64,8,128]{2,1,0:T(8,128)S(1)}, u32[]{:S(2)}, u32[]{:S(2)}) async-start(f32[64,8,128]{2,1,0:T(8,128)} %outer.1), calls=%async_computation.2 | async-start | bytes 524288 | tf_op jit(solution)/shard_map/all_to_all | solution.py:167
  115.0 32.9 %collective-permute-start.5 = (f32[64,512]{1,0:T(8,128)S(1)}, f32[64,512]{1,0:T(8,128)S(1)}, u32[]{:S(2)}, u32[]{:S(2)}) collective-permute-start(f32[64,512]{1,0:T(8,128)S(1)} %add.40), channel_id=1, source_target_pairs={{0,8},{1,9},{2,10},{3,11},{4,12},{5,13},{6,14},{7,15},{8,0},{9,1},... | collective-permute-start | bytes 393224 | tf_op jit(solution)/shard_map/ppermute | solution.py:175
  169.5 21.5 %all-to-all-start.4 = ((f32[64,4,128]{2,1,0:T(4,128)}), f32[64,4,128]{2,1,0:T(4,128)S(1)}, u32[]{:S(2)}, u32[]{:S(2)}) async-start(f32[64,4,128]{2,1,0:T(4,128)} %bitcast.8), calls=%async_computation.4 | async-start | bytes 262144 | tf_op jit(solution)/shard_map/all_to_all | solution.py:167
  176.6 7.8 %collective-permute-start.8 = (f32[64,512]{1,0:T(8,128)S(1)}, f32[64,512]{1,0:T(8,128)S(1)}, u32[]{:S(2)}, u32[]{:S(2)}) collective-permute-start(f32[64,512]{1,0:T(8,128)S(1)} %add.43), channel_id=1, source_target_pairs={{0,384},{128,0},{256,128},{384,256},{1,385},{129,1},{257,129},{385... | collective-permute-start | bytes 393224 | tf_op jit(solution)/shard_map/ppermute | solution.py:256
  179.5 7.5 %collective-permute-start.7 = (f32[64,512]{1,0:T(8,128)S(1)}, f32[64,512]{1,0:T(8,128)S(1)}, u32[]{:S(2)}, u32[]{:S(2)}) collective-permute-start(f32[64,512]{1,0:T(8,128)S(1)} %add.43), channel_id=1, source_target_pairs={{0,256},{128,384},{256,0},{384,128},{1,257},{129,385},{257,1},{385... | collective-permute-start | bytes 393224 | tf_op jit(solution)/shard_map/ppermute | solution.py:256
  182.5 7.4 %collective-permute-start.6 = (f32[64,512]{1,0:T(8,128)S(1)}, f32[64,512]{1,0:T(8,128)S(1)}, u32[]{:S(2)}, u32[]{:S(2)}) collective-permute-start(f32[64,512]{1,0:T(8,128)S(1)} %add.43), channel_id=1, source_target_pairs={{0,128},{128,256},{256,384},{384,0},{1,129},{129,257},{257,385},{3... | collective-permute-start | bytes 393224 | tf_op jit(solution)/shard_map/ppermute | solution.py:256
  191.0 32.9 %collective-permute-start.9 = (f32[4,64,512]{2,1,0:T(8,128)S(1)}, f32[4,64,512]{2,1,0:T(8,128)S(1)}, u32[]{:S(2)}, u32[]{:S(2)}) collective-permute-start(f32[4,64,512]{2,1,0:T(8,128)S(1)} %pad_maximum_fusion.1.gram_ref), channel_id=1, source_target_pairs={{0,64},{64,0},{1,65},{65,1},{2,66},{66,2},{3,67},{67,3},{4,68},{68... | collective-permute-start | bytes 1572872 | tf_op jit(solution)/shard_map/ppermute | solution.py:175
  232.5 6.2 %collective-permute-start.10 = (f32[4,192,128]{2,1,0:T(8,128)S(1)}, f32[4,192,128]{2,1,0:T(8,128)}, u32[]{:S(2)}, u32[]{:S(2)}) collective-permute-start(f32[4,192,128]{2,1,0:T(8,128)S(1)} %all_to_all.37.sums_ref), channel_id=1, source_target_pairs={{0,64},{64,0},{1,65},{65,1},{2,66},{66,2},{3,67},{67,3},{4,68},{68... | collective-permute-start | bytes 1179656 | tf_op jit(solution)/shard_map/ppermute | solution.py:175

commit v3 on v1

--- a/solution.py
+++ b/solution.py
@@ -29,27 +29,38 @@
         wr = [jnp.broadcast_to(ws[p][i:i + 1, :], full) for i in range(8)]
         s = [[jnp.broadcast_to(xr[i][:, base + j:base + j + 1], full) for j in range(i + 1)] for i in range(8)]
         m = [[None] * 8 for _ in range(8)]
-        inv = [None] * 8
-        for k in range(8):
-            inv[k] = 1.0 / s[k][k]
-            for i in range(k + 1, 8):
-                m[i][k] = s[i][k] * inv[k]
-                for j in range(k + 1, i + 1):
-                    s[i][j] = s[i][j] - m[i][k] * s[j][k]
-        for i in range(8):
-            for k in range(i):
-                xr[i] = xr[i] - m[i][k] * xr[k]
-                wr[i] = wr[i] - m[i][k] * wr[k]
-        for i in range(8):
-            w_ref[base + i: base + i + 1, :] = (wr[i] * lax.rsqrt(s[i][i]))[0:1, :]
+        inv = [None] * 4
+        for k in range(0, 8, 2):
+            a, b, d = s[k][k], s[k + 1][k], s[k + 1][k + 1]
+            det = 1.0 / (a * d - b * b)
+            ia, ib, id_ = d * det, b * det, a * det
+            inv[k // 2] = (ia, ib, id_)
+            for i in range(k + 2, 8):
+                m[i][k] = s[i][k] * ia - s[i][k + 1] * ib
+                m[i][k + 1] = s[i][k + 1] * id_ - s[i][k] * ib
+                for j in range(k + 2, i + 1):
+                    s[i][j] = s[i][j] - (m[i][k] * s[j][k] + m[i][k + 1] * s[j][k + 1])
+        for i in range(2, 8):
+            for k in range(0, i - i % 2, 2):
+                xr[i] = xr[i] - (m[i][k] * xr[k] + m[i][k + 1] * xr[k + 1])
+                wr[i] = wr[i] - (m[i][k] * wr[k] + m[i][k + 1] * wr[k + 1])
+        for k in range(0, 8, 2):
+            a, b = s[k][k], s[k + 1][k]
+            w_ref[base + k: base + k + 1, :] = (wr[k] * lax.rsqrt(a))[0:1, :]
+            ratio = b / a
+            low = (wr[k + 1] - ratio * wr[k]) * lax.rsqrt(s[k + 1][k + 1] - ratio * b)
+            w_ref[base + k + 1: base + k + 2, :] = low[0:1, :]
         if p == nb // 8 - 1:
             break
-        xv = [xr[i] * inv[i] for i in range(8)]
-        wv = [wr[i] * inv[i] for i in range(8)]
-        for i in range(7, -1, -1):
-            for k in range(i + 1, 8):
-                xv[i] = xv[i] - m[k][i] * xv[k]
-                wv[i] = wv[i] - m[k][i] * wv[k]
+        xv, wv = [None] * 8, [None] * 8
+        for k in range(6, -1, -2):
+            ia, ib, id_ = inv[k // 2]
+            for rows, out in ((xr, xv), (wr, wv)):
+                out[k] = rows[k] * ia - rows[k + 1] * ib
+                out[k + 1] = rows[k + 1] * id_ - rows[k] * ib
+                for i in range(k + 2, 8):
+                    out[k] = out[k] - m[i][k] * out[i]
+                    out[k + 1] = out[k + 1] - m[i][k + 1] * out[i]
         for q in range(p + 1, nb // 8):
             cols = [jnp.broadcast_to(xs[q][:, base + i:base + i + 1], full) for i in range(8)]
             for i in range(8):
@@ -89,17 +100,21 @@
     )(block, tiles, sketch, gram_rows)
 
 
-def finish_kernel(at_ref, sums_ref, f_ref, s_ref, ns_ref, co_ref, a_ref, x_ref, k_ref, p_ref, d_ref, w_ref):
+def finish_kernel(at_ref, sums_ref, sums2_ref, f_ref, s_ref, ns_ref, co_ref, a_ref, x_ref, k_ref, p_ref, d_ref, w_ref):
     n = a_ref.shape[0]
     own, e = f_ref.shape[1], f_ref.shape[0]
-    blocks = sums_ref.shape[0]
-    rows, cut = e // blocks, n // blocks
-    for b in range(blocks):
-        at = 0
-        for to, height in ((k_ref, rows), (p_ref, rows), (a_ref, cut)):
-            for o in range(0, to.shape[1], 128):
-                to[b * height:(b + 1) * height, o:o + 128] = sums_ref[b, at:at + height, :]
-                at += height
+    across = sums_ref.shape[0]
+    rows, cut = e // (2 * across), n // (2 * across)
+    for side in range(2):
+        core = at_ref[1] if side == 0 else 1 - at_ref[1]
+        sums = sums_ref if side == 0 else sums2_ref
+        for b in range(across):
+            at = 0
+            for to, height in ((k_ref, rows), (p_ref, rows), (a_ref, cut)):
+                place = pl.ds(pl.multiple_of((2 * b + core) * height, height), height)
+                for o in range(0, to.shape[1], 128):
+                    to[place, o:o + 128] = sums[b, at:at + height, :]
+                    at += height
     k = k_ref[...]
     p = p_ref[...]
     er = lax.broadcasted_iota(jnp.int32, (e, e), 0)
@@ -109,8 +124,10 @@
     q = p + mm(k * c, p, ((1,), (0,)))
     x_ref[:own, :] = s_ref[...] + mm(f_ref[...] * c, p, ((0,), (0,)))
     x_ref[own:, :] = q
-    a_ref[...] = a_ref[...] + mm(p * c, p + q, ((0,), (0,)))
-    colid = lax.broadcasted_iota(jnp.int32, (128, n), 1)
+    pq = p + q
+    pc = p * c
+    for o in range(0, n, 128):
+        a_ref[o:o + 128, o:] = a_ref[o:o + 128, o:] + mm(pc[:, o:o + 128], pq[:, o:], ((0,), (0,)))
     ri = lax.broadcasted_iota(jnp.int32, (128, 128), 0)
     ci = lax.broadcasted_iota(jnp.int32, (128, 128), 1)
 
@@ -120,12 +137,14 @@
         w_ref[...] = jnp.where(ri == ci, 1.0, 0.0)
         factor_block(d_ref, w_ref)
         w = w_ref[...]
-        r = mm(w, a_ref[pl.ds(o, 128), :], ((1,), (0,)))
-        r = jnp.where(colid >= o + 128, r, 0.0)
-        y = mm(x_ref[:, pl.ds(o, 128)], w, ((1,), (1,)))
-        x_ref[...] = x_ref[...] - mm(y, r, ((1,), (0,)))
-        x_ref[:, pl.ds(o, 128)] = y
-        a_ref[...] = a_ref[...] - mm(r, r, ((0,), (0,)))
+        x_ref[:, pl.ds(o, 128)] = mm(x_ref[:, pl.ds(o, 128)], w, ((1,), (1,)))
+        for at in range(0, n - 128, 128):
+            @pl.when(b * 128 == at)
+            def _(at=at):
+                r = mm(w, a_ref[at:at + 128, at + 128:], ((1,), (0,)))
+                x_ref[:, at + 128:] = x_ref[:, at + 128:] - mm(x_ref[:, at:at + 128], r, ((1,), (0,)))
+                for o in range(at + 128, n, 128):
+                    a_ref[o:o + 128, o:] = a_ref[o:o + 128, o:] - mm(r[:, o - at - 128:o - at], r[:, o - at - 128:], ((0,), (0,)))
         return carry
 
     lax.fori_loop(0, n // 128, step, 0)
@@ -136,13 +155,13 @@
     co_ref[...] = mine / jnp.sqrt(mean + 1e-6)
 
 
-def finish(at, sums, f, s):
+def finish(at, sums, sums2, f, s):
     n, own, e = s.shape[1], s.shape[0], f.shape[0]
     vmem = pl.BlockSpec(memory_space=pltpu.VMEM)
     return pl.pallas_call(
         finish_kernel,
         out_shape=(jax.ShapeDtypeStruct((own, n), jnp.float32), jax.ShapeDtypeStruct((EX_GROUP, n), jnp.float32)),
-        in_specs=[pl.BlockSpec(memory_space=pltpu.SMEM), vmem, vmem, vmem],
+        in_specs=[pl.BlockSpec(memory_space=pltpu.SMEM)] + [vmem] * 4,
         out_specs=(vmem, vmem),
         scratch_shapes=[
             pltpu.VMEM((n, n), jnp.float32),
@@ -154,7 +173,7 @@
         ],
         compiler_params=pltpu.CompilerParams(vmem_limit_bytes=40 * 1024 * 1024),
         name="finish",
-    )(at, sums, f, s)
+    )(at, sums, sums2, f, s)
 
 
 def exchange(x, axes):
@@ -225,16 +244,18 @@
         ],
         axis=1,
     )
-    parts = exchange(projected.reshape(owners, own_tokens, 2 * width), FS)
+    parts = exchange(projected.reshape(4, -1, 2 * width), "yl")
+    parts = exchange(jnp.sum(parts, axis=0).reshape(-1, own_tokens, 2 * width), "z")
     partial_features = outer(parts, own_segments)
     tile = jnp.sum(exchange(partial_features, FS), axis=0) / count_tile
     tiles = spread(tile, DP)
     sums, features = products(block[None], tiles, sketch, gram_rows)
     chunk = jnp.sum(exchange(sums.reshape(owners, -1, 128), FS), axis=0)
     sums = spread(chunk, FS).reshape(sums.shape)[: 2 * EX_GROUP * 6 + cut * 4]
-    sums = spread(sums, XC)
-    at = block * 2 + lax.axis_index("yh")
-    return finish(at[None], sums, features, sketch)
+    sums = spread(sums, "x")
+    other = lax.ppermute(sums, "c", [(0, 1), (1, 0)])
+    at = jnp.stack([block * 2 + lax.axis_index("yh"), lax.axis_index("c")])
+    return finish(at, sums, other, features, sketch)
 
 
 def solution(mesh):

time: 254 us -> 221 us (0.87)
  waiting for transfers between devices: 102 us -> 42.1 us
  blocking collectives: 51.5 us -> 83.9 us
  Pallas kernels: 40.2 us -> 27.8 us
  starting transfers between devices: 51.4 us -> 60.1 us
    all_to_all x4 -> x3, waiting for transfers between devices: 102 us -> 40.1 us  [exchange(): return lax.all_to_all(x, axes, 0, 0, tiled=True)]
    all_to_all x2 -> x4, blocking collectives: 51.5 us -> 83.9 us  [exchange(): return lax.all_to_all(x, axes, 0, 0, tiled=True)]
    pallas_call x1, Pallas kernels: 38.2 us -> 25.9 us  [finish(): pl.pallas_call(finish_kernel, out_shape=(jax.ShapeDtypeStruct((own, n), j...]
    ppermute x0 -> x1, starting transfers between devices: none -> 6.75 us  [per_device(): other = lax.ppermute(sums, 'c', [(0, 1), (1, 0)])]
    all_to_all x4 -> x3, starting transfers between devices: 51.4 us -> 53.3 us  [exchange(): return lax.all_to_all(x, axes, 0, 0, tiled=True)]
where the time goes in v3:
time: 221 us
  blocking collectives  83.9 us (38%)
  starting transfers between devices  60.1 us (27%)
  waiting for transfers between devices  42.1 us (19%)
  Pallas kernels  27.8 us (13%)
  local copies, waits for them, and re-layouts  3.63 us (2%)
    all_to_all x4, blocking collectives, exchange(): return lax.all_to_all(x, axes, 0, 0, tiled=True)  83.9 us
    all_to_all x3, starting transfers between devices, exchange(): return lax.all_to_all(x, axes, 0, 0, tiled=True)  53.3 us
    all_to_all x3, waiting for transfers between devices, exchange(): return lax.all_to_all(x, axes, 0, 0, tiled=True)  40.1 us
    pallas_call x1, Pallas kernels, finish(): pl.pallas_call(finish_kernel, out_shape=(jax.ShapeDtypeStruct((own, n), j...  25.9 us
    ppermute x1, starting transfers between devices, per_device(): other = lax.ppermute(sums, 'c', [(0, 1), (1, 0)])  6.75 us
  transfers between devices with their start and end apart: 4, of which 4 were waited for; matrix products, arithmetic and copies ran while one was open for 0% of the time, Pallas kernels for 0%

profile of v3, /device:TPU:1, one launch (start us, length us, event | category | flops | bytes accessed | tf_op | source)
XLA Modules:
  0.0 220.8 jit_solution(5200519243890835504)
XLA Ops:
  0.6 0.0 copy-start
  0.6 0.0 copy-start.2
  0.7 0.0 copy-start.3
  0.7 1.5 copy-done
  2.1 1.3 fusion.4
  3.4 0.0 copy-done.2
  3.4 0.0 copy-done.3
  3.4 0.3 fusion.3
  3.7 0.1 pad_maximum_fusion
  3.8 0.1 copy.23
  3.9 0.0 copy-start.4
  3.9 20.0 %all_to_all.35 = f32[4,512,128]{1,2,0:T(8,128)S(1)} all-to-all(f32[4,512,128]{1,2,0:T(8,128)S(1)} %bitcast.22), channel_id=1, replica_groups=mesh['yh'=2,'x'=4,'c'=2,'yl'=4,'z'=16] {'yl'}, dimensions={0} | all-to-all | bytes 2097152 | tf_op jit(solution)/shard_map/all_to_all | solution.py:180
  24.0 0.0 copy-start.1
  24.0 0.1 reduce_sum.36
  24.0 0.8 copy.17
  24.9 28.7 %all-to-all-start.1 = ((f32[16,32,128]{2,1,0:T(8,128)}), f32[16,32,128]{2,1,0:T(8,128)S(1)}, u32[]{:S(2)}, u32[]{:S(2)}) async-start(f32[16,32,128]{2,1,0:T(8,128)} %bitcast.3), calls=%async_computation.1 | async-start | bytes 524288 | tf_op jit(solution)/shard_map/all_to_all | solution.py:180
  53.5 0.0 copy-done.4
  53.6 0.1 dynamic-slice_bitcast_fusion
  53.6 0.1 copy.18.seg_ref
  53.7 12.6 %all-to-all-done.1.part_ref = f32[16,32,128]{2,1,0:T(8,128)S(1)} async-done(((f32[16,32,128]{2,1,0:T(8,128)}), f32[16,32,128]{2,1,0:T(8,128)S(1)}, u32[]{:S(2)}, u32[]{:S(2)}) %all-to-all-start.1) | async-done | bytes 262176 | tf_op jit(solution)/shard_map/all_to_all | solution.py:180
  66.3 1.6 outer.1
  67.9 13.8 %all-to-all-start.2 = ((f32[64,8,128]{2,1,0:T(8,128)}), f32[64,8,128]{2,1,0:T(8,128)S(1)}, u32[]{:S(2)}, u32[]{:S(2)}) async-start(f32[64,8,128]{2,1,0:T(8,128)} %outer.1), calls=%async_computation.2 | async-start | bytes 524288 | tf_op jit(solution)/shard_map/all_to_all | solution.py:180
  81.7 0.1 convert_reduce_fusion
  81.8 0.1 reshape.36
  81.9 0.1 copy.19
  82.0 0.1 broadcast_in_dim.32
  82.0 0.1 reshape.37
  82.1 18.2 %all-to-all-done.2 = f32[64,8,128]{2,1,0:T(8,128)S(1)} async-done(((f32[64,8,128]{2,1,0:T(8,128)}), f32[64,8,128]{2,1,0:T(8,128)S(1)}, u32[]{:S(2)}, u32[]{:S(2)}) %all-to-all-start.2) | async-done | bytes 262176 | tf_op jit(solution)/shard_map/all_to_all | solution.py:180
  100.3 0.1 reduce_sum.37
  100.4 0.6 broadcast_in_dim.33
  101.0 10.9 %all-to-all-start.3 = ((f32[16,8,128]{2,1,0:T(8,128)}), f32[16,8,128]{2,1,0:T(8,128)S(1)}, u32[]{:S(2)}, u32[]{:S(2)}) async-start(f32[16,8,128]{2,1,0:T(8,128)} %broadcast_in_dim.33), calls=%async_computation.3 | async-start | bytes 131072 | tf_op jit(solution)/shard_map/all_to_all | solution.py:180
  111.9 0.0 copy-done.1
  112.0 0.4 fusion.gram_ref
  112.4 9.3 %all-to-all-done.3.tiles_ref = f32[16,8,128]{2,1,0:T(8,128)S(1)} async-done(((f32[16,8,128]{2,1,0:T(8,128)}), f32[16,8,128]{2,1,0:T(8,128)S(1)}, u32[]{:S(2)}, u32[]{:S(2)}) %all-to-all-start.3) | async-done | bytes 65568 | tf_op jit(solution)/shard_map/all_to_all | solution.py:180
  121.7 0.4 products.1
  122.1 25.1 %all_to_all.36 = f32[64,8,128]{2,1,0:T(8,128)S(1)} all-to-all(f32[64,8,128]{2,1,0:T(8,128)S(1)} %bitcast.20), channel_id=1, replica_groups=mesh['yh'=2,'x'=4,'c'=2,'yl'=4,'z'=16] {'yl','z'}, dimensions={0} | all-to-all | bytes 524288 | tf_op jit(solution)/shard_map/all_to_all | solution.py:180
  147.2 0.1 reduce_sum.39
  147.3 26.3 %all_to_all.37 = f32[64,8,128]{2,1,0:T(8,128)S(1)} all-to-all(f32[64,8,128]{2,1,0:T(8,128)S(1)} %broadcast_in_dim.34), channel_id=1, replica_groups=mesh['yh'=2,'x'=4,'c'=2,'yl'=4,'z'=16] {'yl','z'}, dimensions={0} | all-to-all | bytes 524288 | tf_op jit(solution)/shard_map/all_to_all | solution.py:180
  173.6 0.1 broadcast_in_dim.36
  173.7 12.4 %all_to_all.38.sums_ref = f32[4,448,128]{2,1,0:T(8,128)S(1)} all-to-all(f32[4,448,128]{2,1,0:T(8,128)S(1)} %broadcast_in_dim.36), channel_id=1, replica_groups=mesh['yh'=2,'x'=4,'c'=2,'yl'=4,'z'=16] {'x'}, dimensions={0} | all-to-all | bytes 1835008 | tf_op jit(solution)/shard_map/all_to_all | solution.py:180
  186.1 6.7 %collective-permute-start = (f32[4,448,128]{2,1,0:T(8,128)S(1)}, f32[4,448,128]{2,1,0:T(8,128)}, u32[]{:S(2)}, u32[]{:S(2)}) collective-permute-start(f32[4,448,128]{2,1,0:T(8,128)S(1)} %all_to_all.38.sums_ref), channel_id=1, source_target_pairs={{0,64},{64,0},{1,65},{65,1},{2,66},{66,2},{3,67},{67,3},{4,68},{68... | collective-permute-start | bytes 2752520 | tf_op jit(solution)/shard_map/ppermute | solution.py:256
  192.8 0.1 pad_add_fusion.at_ref
  192.9 1.9 collective-permute-done.sums2_ref
  194.9 25.9 %finish.1 = (f32[64,512]{1,0:T(8,128)}, f32[16,512]{1,0:T(8,128)}) custom-call(s32[2]{0:T(128)S(1)} %pad_add_fusion.at_ref, f32[4,448,128]{2,1,0:T(8,128)S(1)} %all_to_all.38.sums_ref, f32[4,448,128]{2,1,0:T(8,128)} %collective-permute-done.sums2_ref, f32[256,64]{1,0:T(8,128)S(1)} %get-tuple-element.5.f_ref, f32[64,512]{1,0:T(8,128)S(1)} %copy-done.1), custom_call_target="tpu_custom_call" | custom-call | tf_op jit(solution)/shard_map/finish/pallas_call | solution.py:161
  (3 shorter events, 0.0 us)
Async XLA Ops:
  0.6 1.5 copy-start
  0.6 2.8 %copy-start.2 = (bf16[2048,128]{1,0:T(8,128)(2,1)S(1)}, bf16[2048,128]{1,0:T(8,128)(2,1)}, u32[]{:S(2)}) copy-start(bf16[2048,128]{1,0:T(8,128)(2,1)} %param.6) | copy-start | bytes 1572868
  0.7 2.8 %copy-start.3 = (bf16[128,64]{0,1:T(8,128)(2,1)S(1)}, bf16[128,64]{0,1:T(8,128)(2,1)}, u32[]{:S(2)}) copy-start(bf16[128,64]{0,1:T(8,128)(2,1)} %param.8) | copy-start | bytes 49156
  3.9 49.6 %copy-start.4 = (s32[1,2048]{1,0:T(1,128)S(1)}, s32[1,2048]{1,0:T(1,128)}, u32[]{:S(2)}) copy-start(s32[1,2048]{1,0:T(1,128)} %param.10) | copy-start | bytes 24580
  24.0 88.0 %copy-start.1 = (f32[64,512]{1,0:T(8,128)S(1)}, f32[64,512]{1,0:T(8,128)}, u32[]{:S(2)}) copy-start(f32[64,512]{1,0:T(8,128)} %s_ref.1) | copy-start | bytes 393220
  24.9 41.5 %all-to-all-start.1 = ((f32[16,32,128]{2,1,0:T(8,128)}), f32[16,32,128]{2,1,0:T(8,128)S(1)}, u32[]{:S(2)}, u32[]{:S(2)}) async-start(f32[16,32,128]{2,1,0:T(8,128)} %bitcast.3), calls=%async_computation.1 | async-start | bytes 524288 | tf_op jit(solution)/shard_map/all_to_all | solution.py:180
  67.9 32.4 %all-to-all-start.2 = ((f32[64,8,128]{2,1,0:T(8,128)}), f32[64,8,128]{2,1,0:T(8,128)S(1)}, u32[]{:S(2)}, u32[]{:S(2)}) async-start(f32[64,8,128]{2,1,0:T(8,128)} %outer.1), calls=%async_computation.2 | async-start | bytes 524288 | tf_op jit(solution)/shard_map/all_to_all | solution.py:180
  101.0 20.6 %all-to-all-start.3 = ((f32[16,8,128]{2,1,0:T(8,128)}), f32[16,8,128]{2,1,0:T(8,128)S(1)}, u32[]{:S(2)}, u32[]{:S(2)}) async-start(f32[16,8,128]{2,1,0:T(8,128)} %broadcast_in_dim.33), calls=%async_computation.3 | async-start | bytes 131072 | tf_op jit(solution)/shard_map/all_to_all | solution.py:180
  186.1 8.8 %collective-permute-start = (f32[4,448,128]{2,1,0:T(8,128)S(1)}, f32[4,448,128]{2,1,0:T(8,128)}, u32[]{:S(2)}, u32[]{:S(2)}) collective-permute-start(f32[4,448,128]{2,1,0:T(8,128)S(1)} %all_to_all.38.sums_ref), channel_id=1, source_target_pairs={{0,64},{64,0},{1,65},{65,1},{2,66},{66,2},{3,67},{67,3},{4,68},{68... | collective-permute-start | bytes 2752520 | tf_op jit(solution)/shard_map/ppermute | solution.py:256

commit v4 on v3

--- a/solution.py
+++ b/solution.py
@@ -12,7 +12,9 @@
 EX_GROUP = 16
 DP = ("yh", "x", "c")
 XC = ("x", "c")
-FS = ("yl", "z")
+FS = ("yl", "zh", "zl")
+NEAR = ("yl", "zl")
+FAR = ("zh",)
 
 
 def mm(a, b, dims, prec=HI):
@@ -92,7 +94,7 @@
     vmem = pl.BlockSpec(memory_space=pltpu.VMEM)
     return pl.pallas_call(
         products_kernel,
-        out_shape=(jax.ShapeDtypeStruct((512, 128), jnp.float32), jax.ShapeDtypeStruct((256, 64), jnp.float32)),
+        out_shape=(jax.ShapeDtypeStruct((384, 128), jnp.float32), jax.ShapeDtypeStruct((256, 64), jnp.float32)),
         in_specs=[pl.BlockSpec(memory_space=pltpu.SMEM), vmem, vmem, vmem],
         out_specs=(vmem, vmem),
         compiler_params=pltpu.CompilerParams(vmem_limit_bytes=24 * 1024 * 1024),
@@ -100,17 +102,17 @@
     )(block, tiles, sketch, gram_rows)
 
 
-def finish_kernel(at_ref, sums_ref, sums2_ref, f_ref, s_ref, ns_ref, co_ref, a_ref, x_ref, k_ref, p_ref, d_ref, w_ref):
+def finish_kernel(at_ref, sums_ref, sums2_ref, f_ref, s_ref, ns_ref, co_ref, a_ref, x_ref, k_ref, p_ref, g_ref, d_ref, w_ref):
     n = a_ref.shape[0]
     own, e = f_ref.shape[1], f_ref.shape[0]
     across = sums_ref.shape[0]
-    rows, cut = e // (2 * across), n // (2 * across)
+    rows, cut = e // (2 * across), g_ref.shape[0] // (2 * across)
     for side in range(2):
         core = at_ref[1] if side == 0 else 1 - at_ref[1]
         sums = sums_ref if side == 0 else sums2_ref
         for b in range(across):
             at = 0
-            for to, height in ((k_ref, rows), (p_ref, rows), (a_ref, cut)):
+            for to, height in ((k_ref, rows), (p_ref, rows), (g_ref, cut)):
                 place = pl.ds(pl.multiple_of((2 * b + core) * height, height), height)
                 for o in range(0, to.shape[1], 128):
                     to[place, o:o + 128] = sums[b, at:at + height, :]
@@ -126,8 +128,12 @@
     x_ref[own:, :] = q
     pq = p + q
     pc = p * c
+    at = 0
     for o in range(0, n, 128):
-        a_ref[o:o + 128, o:] = a_ref[o:o + 128, o:] + mm(pc[:, o:o + 128], pq[:, o:], ((0,), (0,)))
+        update = mm(pc[:, o:o + 128], pq[:, o:], ((0,), (0,)))
+        for to in range(o, n, 128):
+            a_ref[o:o + 128, to:to + 128] = g_ref[at:at + 128, :] + update[:, to - o:to - o + 128]
+            at += 128
     ri = lax.broadcasted_iota(jnp.int32, (128, 128), 0)
     ci = lax.broadcasted_iota(jnp.int32, (128, 128), 1)
 
@@ -168,6 +174,7 @@
             pltpu.VMEM((own + e, n), jnp.float32),
             pltpu.VMEM((e, e), jnp.float32),
             pltpu.VMEM((e, n), jnp.float32),
+            pltpu.VMEM((n * (n + 128) // 256, 128), jnp.float32),
             pltpu.VMEM((128, 128), jnp.float32),
             pltpu.VMEM((128, 128), jnp.float32),
         ],
@@ -225,11 +232,13 @@
     rank = sketch.shape[1]
     half = EX_GROUP // 2
     own_tokens = tokens // owners
-    place = lax.axis_index(FS)
+    place = lax.axis_index(NEAR + FAR)
     block = lax.axis_index(XC)
 
-    cut = rank // blocks
-    gram_rows = mm(lax.dynamic_slice_in_dim(sketch, block * cut, cut, 1), sketch, ((0,), (0,)))
+    gram = mm(sketch, sketch, ((0,), (0,)))
+    upper = [gram[o:o + 128, to:to + 128] for o in range(0, rank, 128) for to in range(o, rank, 128)]
+    cut = len(upper) * 128 // blocks
+    gram_rows = lax.dynamic_slice_in_dim(jnp.concatenate(upper, axis=0), block * cut, cut, 0)
 
     segments = segment_ids[0]
     onehot = segments[:, None] == jnp.arange(EX_GROUP, dtype=jnp.int32)[None, :]
@@ -244,14 +253,14 @@
         ],
         axis=1,
     )
-    parts = exchange(projected.reshape(4, -1, 2 * width), "yl")
-    parts = exchange(jnp.sum(parts, axis=0).reshape(-1, own_tokens, 2 * width), "z")
+    parts = exchange(projected.reshape(lax.axis_size(NEAR), -1, 2 * width), NEAR)
+    parts = exchange(jnp.sum(parts, axis=0).reshape(-1, own_tokens, 2 * width), FAR)
     partial_features = outer(parts, own_segments)
     tile = jnp.sum(exchange(partial_features, FS), axis=0) / count_tile
     tiles = spread(tile, DP)
     sums, features = products(block[None], tiles, sketch, gram_rows)
-    chunk = jnp.sum(exchange(sums.reshape(owners, -1, 128), FS), axis=0)
-    sums = spread(chunk, FS).reshape(sums.shape)[: 2 * EX_GROUP * 6 + cut * 4]
+    chunk = jnp.sum(exchange(sums.reshape(owners, 1, -1), FS), axis=0)
+    sums = spread(chunk, FS).reshape(sums.shape)[: 2 * EX_GROUP * 6 + cut]
     sums = spread(sums, "x")
     other = lax.ppermute(sums, "c", [(0, 1), (1, 0)])
     at = jnp.stack([block * 2 + lax.axis_index("yh"), lax.axis_index("c")])
@@ -259,7 +268,7 @@
 
 
 def solution(mesh):
-    fine = Mesh(mesh.devices.reshape(2, 4, 2, 4, 16), ("yh", "x", "c", "yl", "z"))
+    fine = Mesh(mesh.devices.reshape(2, 4, 2, 4, 4, 4), ("yh", "x", "c", "yl", "zh", "zl"))
     return jax.shard_map(
         per_device,
         mesh=fine,

time: 221 us -> 212 us (0.959)
  blocking collectives: 83.9 us -> 57.7 us
  waiting for transfers between devices: 42.1 us -> 57.9 us
  starting transfers between devices: 60.1 us -> 52.7 us
  local copies, waits for them, and re-layouts: 3.63 us -> 8.84 us
  other arithmetic: 0.53 us -> 2.85 us
    all_to_all x4 -> x3, blocking collectives: 83.9 us -> 57.7 us  [exchange(): return lax.all_to_all(x, axes, 0, 0, tiled=True)]
    all_to_all x3 -> x4, waiting for transfers between devices: 40.1 us -> 56.4 us  [exchange(): return lax.all_to_all(x, axes, 0, 0, tiled=True)]
    all_to_all x3 -> x4, starting transfers between devices: 53.3 us -> 46.8 us  [exchange(): return lax.all_to_all(x, axes, 0, 0, tiled=True)]
    unnamed x10 -> x14, local copies, waits for them, and re-layouts: 1.5 us -> 5.26 us
  transfers between devices with their start and end apart: 4 -> 5, of which waited for: 4 -> 5; matrix products, arithmetic and copies ran while one was open for 0% -> 4% of each run, Pallas kernels for 0% -> 0%
where the time goes in v4:
time: 212 us
  waiting for transfers between devices  57.9 us (27%)
  blocking collectives  57.7 us (27%)
  starting transfers between devices  52.7 us (25%)
  Pallas kernels  27.1 us (13%)
  local copies, waits for them, and re-layouts  8.84 us (4%)
  matrix products  3.77 us (2%)
  other arithmetic  2.85 us (1%)
    all_to_all x3, blocking collectives, exchange(): return lax.all_to_all(x, axes, 0, 0, tiled=True)  57.7 us
    all_to_all x4, waiting for transfers between devices, exchange(): return lax.all_to_all(x, axes, 0, 0, tiled=True)  56.4 us
    all_to_all x4, starting transfers between devices, exchange(): return lax.all_to_all(x, axes, 0, 0, tiled=True)  46.8 us
    pallas_call x1, Pallas kernels, finish(): pl.pallas_call(finish_kernel, out_shape=(jax.ShapeDtypeStruct((own, n), j...  25.2 us
    ppermute x1, starting transfers between devices, per_device(): other = lax.ppermute(sums, 'c', [(0, 1), (1, 0)])  5.92 us
    unnamed x14, local copies, waits for them, and re-layouts  5.26 us
  transfers between devices with their start and end apart: 5, of which 5 were waited for; matrix products, arithmetic and copies ran while one was open for 4% of the time, Pallas kernels for 0%

profile of v4, /device:TPU:1, one launch (start us, length us, event | category | flops | bytes accessed | tf_op | source)
XLA Modules:
  0.0 211.7 jit_solution(9812679240086368608)
XLA Ops:
  0.6 0.0 copy-start
  0.6 1.5 fusion
  2.1 0.2 copy-done
  2.3 1.3 fusion.2
  3.6 0.0 copy-start.2
  3.6 0.0 copy-start.1
  3.6 1.1 copy_bitcast_fusion
  4.7 11.0 %all-to-all-start = ((f32[16,128,128]{1,2,0:T(8,128)}), f32[16,128,128]{1,2,0:T(8,128)}, u32[]{:S(2)}, u32[]{:S(2)}) async-start(f32[16,128,128]{1,2,0:T(8,128)} %copy_bitcast_fusion), calls=%async_computation | async-start | bytes 2097152 | tf_op jit(solution)/shard_map/all_to_all | solution.py:187
  15.8 0.0 copy-done.2
  15.8 0.1 dynamic-slice_bitcast_fusion
  15.9 0.1 copy.19.seg_ref
  15.9 0.1 convert_reduce_fusion
  16.1 0.1 reshape.40
  16.2 0.1 copy.20
  16.2 0.1 broadcast_in_dim.14
  16.3 0.1 reshape.41
  16.4 0.0 copy-done.1
  16.4 1.0 fusion.1
  17.4 0.6 slice_dynamic-update-slice_fusion.8
  18.1 0.6 slice_dynamic-update-slice_fusion.7
  18.7 23.3 %all-to-all-done = f32[16,128,128]{1,2,0:T(8,128)} async-done(((f32[16,128,128]{1,2,0:T(8,128)}), f32[16,128,128]{1,2,0:T(8,128)}, u32[]{:S(2)}, u32[]{:S(2)}) %all-to-all-start) | async-done | bytes 1048608 | tf_op jit(solution)/shard_map/all_to_all | solution.py:187
  42.1 1.3 reduce_sum.36
  43.3 0.7 copy.18
  44.1 19.3 %all-to-all-start.1 = ((f32[4,32,128]{2,1,0:T(8,128)}), f32[4,32,128]{2,1,0:T(8,128)S(1)}, u32[]{:S(2)}, u32[]{:S(2)}) async-start(f32[4,32,128]{2,1,0:T(8,128)} %bitcast.3), calls=%async_computation.1 | async-start | bytes 131072 | tf_op jit(solution)/shard_map/all_to_all | solution.py:187
  63.3 0.6 slice_dynamic-update-slice_fusion.6
  64.0 11.1 %all-to-all-done.1.part_ref = f32[4,32,128]{2,1,0:T(8,128)S(1)} async-done(((f32[4,32,128]{2,1,0:T(8,128)}), f32[4,32,128]{2,1,0:T(8,128)S(1)}, u32[]{:S(2)}, u32[]{:S(2)}) %all-to-all-start.1) | async-done | bytes 65568 | tf_op jit(solution)/shard_map/all_to_all | solution.py:187
  75.0 1.5 outer.1
  76.6 4.6 %all-to-all-start.2 = ((f32[64,8,128]{2,1,0:T(8,128)}), f32[64,8,128]{2,1,0:T(8,128)S(1)}, u32[]{:S(2)}, u32[]{:S(2)}) async-start(f32[64,8,128]{2,1,0:T(8,128)} %outer.1), calls=%async_computation.2 | async-start | bytes 524288 | tf_op jit(solution)/shard_map/all_to_all | solution.py:187
  81.2 0.6 slice_dynamic-update-slice_fusion.5
  81.8 0.6 slice_dynamic-update-slice_fusion.4
  82.5 0.6 slice_dynamic-update-slice_fusion.3
  83.1 0.6 slice_dynamic-update-slice_fusion.2
  83.7 0.6 slice_dynamic-update-slice_fusion.1
  84.4 13.8 %all-to-all-done.2 = f32[64,8,128]{2,1,0:T(8,128)S(1)} async-done(((f32[64,8,128]{2,1,0:T(8,128)}), f32[64,8,128]{2,1,0:T(8,128)S(1)}, u32[]{:S(2)}, u32[]{:S(2)}) %all-to-all-start.2) | async-done | bytes 262176 | tf_op jit(solution)/shard_map/all_to_all | solution.py:187
  98.2 0.1 reduce_sum.37
  98.3 0.6 broadcast_in_dim.15
  98.9 11.9 %all-to-all-start.3 = ((f32[16,8,128]{2,1,0:T(8,128)}), f32[16,8,128]{2,1,0:T(8,128)S(1)}, u32[]{:S(2)}, u32[]{:S(2)}) async-start(f32[16,8,128]{2,1,0:T(8,128)} %broadcast_in_dim.15), calls=%async_computation.3 | async-start | bytes 131072 | tf_op jit(solution)/shard_map/all_to_all | solution.py:187
  110.8 0.7 slice_dynamic-update-slice_fusion
  111.4 0.9 constant_dynamic-slice_fusion.gram_ref
  112.3 8.2 %all-to-all-done.3.tiles_ref = f32[16,8,128]{2,1,0:T(8,128)S(1)} async-done(((f32[16,8,128]{2,1,0:T(8,128)}), f32[16,8,128]{2,1,0:T(8,128)S(1)}, u32[]{:S(2)}, u32[]{:S(2)}) %all-to-all-start.3) | async-done | bytes 65568 | tf_op jit(solution)/shard_map/all_to_all | solution.py:187
  120.5 0.4 products.1
  120.9 22.8 %all_to_all.35 = f32[64,1,768]{2,1,0:T(1,128)S(1)} all-to-all(f32[64,1,768]{2,1,0:T(1,128)S(1)} %bitcast.21), channel_id=1, replica_groups=mesh['yh'=2,'x'=4,'c'=2,'yl'=4,'zh'=4,'zl'=4] {'yl','zh','zl'}, dimensions={0} | all-to-all | bytes 393216 | tf_op jit(solution)/shard_map/all_to_all | solution.py:187
  143.7 0.1 reduce_sum.39
  143.9 0.1 broadcast_in_dim.32
  144.0 23.8 %all_to_all.36 = f32[64,1,768]{2,1,0:T(1,128)S(1)} all-to-all(f32[64,1,768]{2,1,0:T(1,128)S(1)} %broadcast_in_dim.32), channel_id=1, replica_groups=mesh['yh'=2,'x'=4,'c'=2,'yl'=4,'zh'=4,'zl'=4] {'yl','zh','zl'}, dimensions={0} | all-to-all | bytes 393216 | tf_op jit(solution)/shard_map/all_to_all | solution.py:187
  167.8 11.1 %all_to_all.37.sums_ref = f32[4,352,128]{2,1,0:T(8,128)S(1)} all-to-all(f32[4,352,128]{2,1,0:T(8,128)S(1)} %broadcast_in_dim.33), channel_id=1, replica_groups=mesh['yh'=2,'x'=4,'c'=2,'yl'=4,'zh'=4,'zl'=4] {'x'}, dimensions={0} | all-to-all | bytes 1441792 | tf_op jit(solution)/shard_map/all_to_all | solution.py:187
  178.9 5.9 %collective-permute-start = (f32[4,352,128]{2,1,0:T(8,128)S(1)}, f32[4,352,128]{2,1,0:T(8,128)S(1)}, u32[]{:S(2)}, u32[]{:S(2)}) collective-permute-start(f32[4,352,128]{2,1,0:T(8,128)S(1)} %all_to_all.37.sums_ref), channel_id=1, source_target_pairs={{0,64},{64,0},{1,65},{65,1},{2,66},{66,2},{3,67},{67,3},{4,68},{68... | collective-permute-start | bytes 2162696 | tf_op jit(solution)/shard_map/ppermute | solution.py:265
  184.9 0.1 pad_add_fusion.at_ref
  184.9 1.5 collective-permute-done.sums2_ref
  186.5 25.2 %finish.1 = (f32[64,512]{1,0:T(8,128)}, f32[16,512]{1,0:T(8,128)}) custom-call(s32[2]{0:T(128)S(1)} %pad_add_fusion.at_ref, f32[4,352,128]{2,1,0:T(8,128)S(1)} %all_to_all.37.sums_ref, f32[4,352,128]{2,1,0:T(8,128)S(1)} %collective-permute-done.sums2_ref, f32[256,64]{1,0:T(8,128)S(1)} %get-tuple-element.5.f_ref, f32[64,512]{1,0:T(8,128)S(1)} %copy-done.1), custom_call_target="tpu_custom_call" | custom-call | tf_op jit(solution)/shard_map/finish/pallas_call | solution.py:167
  (3 shorter events, 0.1 us)
Async XLA Ops:
  0.6 1.7 copy-start
  3.6 12.2 %copy-start.2 = (s32[1,2048]{1,0:T(1,128)S(1)}, s32[1,2048]{1,0:T(1,128)}, u32[]{:S(2)}) copy-start(s32[1,2048]{1,0:T(1,128)} %param.10) | copy-start | bytes 24580
  3.6 12.8 %copy-start.1 = (f32[64,512]{1,0:T(8,128)S(1)}, f32[64,512]{1,0:T(8,128)}, u32[]{:S(2)}) copy-start(f32[64,512]{1,0:T(8,128)} %s_ref.1) | copy-start | bytes 393220
  4.7 37.3 %all-to-all-start = ((f32[16,128,128]{1,2,0:T(8,128)}), f32[16,128,128]{1,2,0:T(8,128)}, u32[]{:S(2)}, u32[]{:S(2)}) async-start(f32[16,128,128]{1,2,0:T(8,128)} %copy_bitcast_fusion), calls=%async_computation | async-start | bytes 2097152 | tf_op jit(solution)/shard_map/all_to_all | solution.py:187
  44.1 31.0 %all-to-all-start.1 = ((f32[4,32,128]{2,1,0:T(8,128)}), f32[4,32,128]{2,1,0:T(8,128)S(1)}, u32[]{:S(2)}, u32[]{:S(2)}) async-start(f32[4,32,128]{2,1,0:T(8,128)} %bitcast.3), calls=%async_computation.1 | async-start | bytes 131072 | tf_op jit(solution)/shard_map/all_to_all | solution.py:187
  76.6 21.6 %all-to-all-start.2 = ((f32[64,8,128]{2,1,0:T(8,128)}), f32[64,8,128]{2,1,0:T(8,128)S(1)}, u32[]{:S(2)}, u32[]{:S(2)}) async-start(f32[64,8,128]{2,1,0:T(8,128)} %outer.1), calls=%async_computation.2 | async-start | bytes 524288 | tf_op jit(solution)/shard_map/all_to_all | solution.py:187
  98.9 21.6 %all-to-all-start.3 = ((f32[16,8,128]{2,1,0:T(8,128)}), f32[16,8,128]{2,1,0:T(8,128)S(1)}, u32[]{:S(2)}, u32[]{:S(2)}) async-start(f32[16,8,128]{2,1,0:T(8,128)} %broadcast_in_dim.15), calls=%async_computation.3 | async-start | bytes 131072 | tf_op jit(solution)/shard_map/all_to_all | solution.py:187
  178.9 7.5 %collective-permute-start = (f32[4,352,128]{2,1,0:T(8,128)S(1)}, f32[4,352,128]{2,1,0:T(8,128)S(1)}, u32[]{:S(2)}, u32[]{:S(2)}) collective-permute-start(f32[4,352,128]{2,1,0:T(8,128)S(1)} %all_to_all.37.sums_ref), channel_id=1, source_target_pairs={{0,64},{64,0},{1,65},{65,1},{2,66},{66,2},{3,67},{67,3},{4,68},{68... | collective-permute-start | bytes 2162696 | tf_op jit(solution)/shard_map/ppermute | solution.py:265

commit v5 on v4

--- a/solution.py
+++ b/solution.py
@@ -191,6 +191,50 @@
     return exchange(jnp.broadcast_to(x[None], (lax.axis_size(axes),) + x.shape), axes)
 
 
+def project_kernel(x_ref, y_ref, px_ref, py_ref, out_ref):
+    left = lax.dot_general(px_ref[...], x_ref[...], (((1,), (1,)), ((), ())), preferred_element_type=jnp.float32)
+    right = lax.dot_general(py_ref[...], y_ref[...], (((1,), (0,)), ((), ())), preferred_element_type=jnp.float32)
+    width = left.shape[0]
+    for c in range(out_ref.shape[0]):
+        out_ref[c, :width, :] = left[:, c * 128:(c + 1) * 128]
+        out_ref[c, width:, :] = right[:, c * 128:(c + 1) * 128]
+
+
+def project(x, y, px, py):
+    tokens, width = x.shape[0], px.shape[1]
+    step = tokens // 4
+    return pl.pallas_call(
+        project_kernel,
+        grid=(4,),
+        out_shape=jax.ShapeDtypeStruct((tokens // 128, 2 * width, 128), jnp.float32),
+        in_specs=[
+            pl.BlockSpec((step, x.shape[1]), lambda i: (i, 0)),
+            pl.BlockSpec((y.shape[1], step), lambda i: (0, i)),
+            pl.BlockSpec((width, x.shape[1]), lambda i: (0, 0)),
+            pl.BlockSpec((width, y.shape[1]), lambda i: (0, 0)),
+        ],
+        out_specs=pl.BlockSpec((step // 128, 2 * width, 128), lambda i: (i, 0, 0)),
+        compiler_params=pltpu.CompilerParams(vmem_limit_bytes=16 * 1024 * 1024),
+        name="project",
+    )(x, y.T, px.T, py.T)
+
+
+def fold_kernel(parts_ref, out_ref):
+    out_ref[...] = jnp.sum(parts_ref[...], axis=0).T
+
+
+def fold(parts):
+    vmem = pl.BlockSpec(memory_space=pltpu.VMEM)
+    return pl.pallas_call(
+        fold_kernel,
+        out_shape=jax.ShapeDtypeStruct((parts.shape[2], parts.shape[1]), jnp.float32),
+        in_specs=[vmem],
+        out_specs=vmem,
+        compiler_params=pltpu.CompilerParams(vmem_limit_bytes=16 * 1024 * 1024),
+        name="fold",
+    )(parts)
+
+
 def outer_kernel(part_ref, seg_ref, out_ref):
     both = jnp.sum(part_ref[...], axis=0)
     tokens, width = both.shape[0], both.shape[1] // 2
@@ -246,21 +290,15 @@
     count_tile = jnp.repeat(counts.reshape(2, half).T, width, axis=1)
     own_segments = lax.dynamic_slice_in_dim(segments, place * own_tokens, own_tokens, 0)[:, None]
 
-    projected = jnp.concatenate(
-        [
-            jnp.dot(inputs, proj_in, preferred_element_type=jnp.float32),
-            jnp.dot(out_grads, proj_out, preferred_element_type=jnp.float32),
-        ],
-        axis=1,
-    )
-    parts = exchange(projected.reshape(lax.axis_size(NEAR), -1, 2 * width), NEAR)
-    parts = exchange(jnp.sum(parts, axis=0).reshape(-1, own_tokens, 2 * width), FAR)
+    parts = fold(exchange(project(inputs, out_grads, proj_in, proj_out), NEAR))
+    parts = exchange(parts.reshape(-1, own_tokens, 2 * width), FAR)
     partial_features = outer(parts, own_segments)
     tile = jnp.sum(exchange(partial_features, FS), axis=0) / count_tile
     tiles = spread(tile, DP)
     sums, features = products(block[None], tiles, sketch, gram_rows)
-    chunk = jnp.sum(exchange(sums.reshape(owners, 1, -1), FS), axis=0)
-    sums = spread(chunk, FS).reshape(sums.shape)[: 2 * EX_GROUP * 6 + cut]
+    chunk = jnp.sum(exchange(sums.reshape(lax.axis_size(NEAR), -1, 128), NEAR), axis=0)
+    chunk = jnp.sum(spread(chunk, FAR), axis=0)
+    sums = spread(chunk, NEAR).reshape(sums.shape)[: 2 * EX_GROUP * 6 + cut]
     sums = spread(sums, "x")
     other = lax.ppermute(sums, "c", [(0, 1), (1, 0)])
     at = jnp.stack([block * 2 + lax.axis_index("yh"), lax.axis_index("c")])

time: 212 us -> 208 us (0.981)
  blocking collectives: 57.7 us -> 51.3 us
  waiting for transfers between devices: 57.9 us -> 64.3 us
  local copies, waits for them, and re-layouts: 8.84 us -> 5.43 us
  Pallas kernels: 27.1 us -> 30.2 us
  matrix products: 3.77 us -> 1.04 us
  other arithmetic: 2.85 us -> 0.31 us
    all_to_all x3 -> x4, blocking collectives: 57.7 us -> 51.3 us  [exchange(): return lax.all_to_all(x, axes, 0, 0, tiled=True)]
    all_to_all x4, waiting for transfers between devices: 56.4 us -> 62.8 us  [exchange(): return lax.all_to_all(x, axes, 0, 0, tiled=True)]
    pallas_call x0 -> x2, Pallas kernels: none -> 3.03 us  [the longest x1 2.28 us: project(): pl.pallas_call(project_kernel, grid=(4,), out_shape=jax.ShapeDtypeStruct(...]
    dot_general x2 -> x0, matrix products: 2.74 us -> none  [the longest x1 1.47 us: per_device(): jnp.dot(inputs, proj_in, preferred_element_type=jnp.float32)]
    unnamed x14 -> x20, local copies, waits for them, and re-layouts: 5.26 us -> 4.18 us
  transfers between devices with their start and end apart: 5 -> 5, of which waited for: 5 -> 5; matrix products, arithmetic and copies ran while one was open for 4% -> 1% of each run, Pallas kernels for 0% -> 0%
where the time goes in v5:
time: 208 us; the launch traced here: 207 us
  waiting for transfers between devices  64.3 us (31%)
  starting transfers between devices  53.6 us (26%)
  blocking collectives  51.3 us (25%)
  Pallas kernels  30.2 us (15%)
  local copies, waits for them, and re-layouts  5.43 us (3%)
    all_to_all x4, waiting for transfers between devices, exchange(): return lax.all_to_all(x, axes, 0, 0, tiled=True)  62.8 us
    all_to_all x4, blocking collectives, exchange(): return lax.all_to_all(x, axes, 0, 0, tiled=True)  51.3 us
    all_to_all x4, starting transfers between devices, exchange(): return lax.all_to_all(x, axes, 0, 0, tiled=True)  46.9 us
    pallas_call x1, Pallas kernels, finish(): pl.pallas_call(finish_kernel, out_shape=(jax.ShapeDtypeStruct((own, n), j...  25.2 us
    ppermute x1, starting transfers between devices, per_device(): other = lax.ppermute(sums, 'c', [(0, 1), (1, 0)])  6.73 us
    unnamed x20, local copies, waits for them, and re-layouts  4.18 us
  transfers between devices with their start and end apart: 5, of which 5 were waited for; matrix products, arithmetic and copies ran while one was open for 1% of the time, Pallas kernels for 0%

profile of v5, /device:TPU:1, one launch (start us, length us, event | category | flops | bytes accessed | tf_op | source)
XLA Modules:
  0.0 206.9 jit_solution(14489238056296585528)
XLA Ops:
  0.6 0.0 copy-start.1
  0.6 1.5 copy-done.1
  2.1 0.0 copy-start.2
  2.1 1.0 copy-done.2
  3.2 0.0 copy-start.3
  3.2 0.8 copy-done.3
  4.0 0.0 copy-start.4
  4.0 0.7 copy-done.4
  4.7 2.3 %project.1 = f32[16,128,128]{2,1,0:T(8,128)} custom-call(bf16[2048,128]{1,0:T(8,128)(2,1)S(1)} %copy-done.2, bf16[448,2048]{1,0:T(8,128)(2,1)S(1)} %bitcast.15, bf16[64,128]{1,0:T(8,128)(2,1)S(1)} %bitcast.18, bf16[64,448]{1,0:T(8,128)(2,1)S(1)} %bitcast.17), custom_call_target="tpu_custom_call" | custom-call | tf_op jit(solution)/shard_map/project/pallas_call | solution.py:206
  7.0 0.0 copy-start.5
  7.0 0.0 copy-start
  7.0 11.1 %all-to-all-start = ((f32[16,128,128]{2,1,0:T(8,128)}), f32[16,128,128]{2,1,0:T(8,128)S(1)}, u32[]{:S(2)}, u32[]{:S(2)}) async-start(f32[16,128,128]{2,1,0:T(8,128)} %project.1), calls=%async_computation | async-start | bytes 2097152 | tf_op jit(solution)/shard_map/all_to_all | solution.py:187
  18.1 0.0 copy-done.5
  18.1 0.1 dynamic-slice_bitcast_fusion
  18.2 0.1 copy.10.seg_ref
  18.3 0.1 convert_reduce_fusion
  18.4 0.1 reshape.33
  18.5 0.1 copy.11
  18.6 0.1 broadcast_in_dim.16
  18.7 0.1 reshape.34
  18.8 0.0 copy-done
  18.8 1.0 fusion
  19.8 24.5 %all-to-all-done.parts_ref = f32[16,128,128]{2,1,0:T(8,128)S(1)} async-done(((f32[16,128,128]{2,1,0:T(8,128)}), f32[16,128,128]{2,1,0:T(8,128)S(1)}, u32[]{:S(2)}, u32[]{:S(2)}) %all-to-all-start) | async-done | bytes 1048608 | tf_op jit(solution)/shard_map/all_to_all | solution.py:187
  44.4 0.8 fold.1
  45.1 19.3 %all-to-all-start.1 = ((f32[4,32,128]{2,1,0:T(8,128)}), f32[4,32,128]{2,1,0:T(8,128)S(1)}, u32[]{:S(2)}, u32[]{:S(2)}) async-start(f32[4,32,128]{2,1,0:T(8,128)} %bitcast.6), calls=%async_computation.1 | async-start | bytes 131072 | tf_op jit(solution)/shard_map/all_to_all | solution.py:187
  64.4 11.7 %all-to-all-done.1.part_ref = f32[4,32,128]{2,1,0:T(8,128)S(1)} async-done(((f32[4,32,128]{2,1,0:T(8,128)}), f32[4,32,128]{2,1,0:T(8,128)S(1)}, u32[]{:S(2)}, u32[]{:S(2)}) %all-to-all-start.1) | async-done | bytes 65568 | tf_op jit(solution)/shard_map/all_to_all | solution.py:187
  76.1 1.6 outer.1
  77.6 4.6 %all-to-all-start.2 = ((f32[64,8,128]{2,1,0:T(8,128)}), f32[64,8,128]{2,1,0:T(8,128)S(1)}, u32[]{:S(2)}, u32[]{:S(2)}) async-start(f32[64,8,128]{2,1,0:T(8,128)} %outer.1), calls=%async_computation.2 | async-start | bytes 524288 | tf_op jit(solution)/shard_map/all_to_all | solution.py:187
  82.4 16.9 %all-to-all-done.2 = f32[64,8,128]{2,1,0:T(8,128)S(1)} async-done(((f32[64,8,128]{2,1,0:T(8,128)}), f32[64,8,128]{2,1,0:T(8,128)S(1)}, u32[]{:S(2)}, u32[]{:S(2)}) %all-to-all-start.2) | async-done | bytes 262176 | tf_op jit(solution)/shard_map/all_to_all | solution.py:187
  99.2 0.1 reduce_sum.36
  99.3 0.6 broadcast_in_dim.17
  100.0 11.9 %all-to-all-start.3 = ((f32[16,8,128]{2,1,0:T(8,128)}), f32[16,8,128]{2,1,0:T(8,128)S(1)}, u32[]{:S(2)}, u32[]{:S(2)}) async-start(f32[16,8,128]{2,1,0:T(8,128)} %broadcast_in_dim.17), calls=%async_computation.3 | async-start | bytes 131072 | tf_op jit(solution)/shard_map/all_to_all | solution.py:187
  111.9 9.7 %all-to-all-done.3.tiles_ref = f32[16,8,128]{2,1,0:T(8,128)S(1)} async-done(((f32[16,8,128]{2,1,0:T(8,128)}), f32[16,8,128]{2,1,0:T(8,128)S(1)}, u32[]{:S(2)}, u32[]{:S(2)}) %all-to-all-start.3) | async-done | bytes 65568 | tf_op jit(solution)/shard_map/all_to_all | solution.py:187
  121.6 0.4 products.1
  121.9 12.8 %all_to_all.40 = f32[16,24,128]{2,1,0:T(8,128)S(1)} all-to-all(f32[16,24,128]{2,1,0:T(8,128)S(1)} %bitcast.16), channel_id=1, replica_groups=mesh['yh'=2,'x'=4,'c'=2,'yl'=4,'zh'=4,'zl'=4] {'yl','zl'}, dimensions={0} | all-to-all | bytes 393216 | tf_op jit(solution)/shard_map/all_to_all | solution.py:187
  134.8 15.3 %all_to_all.41 = f32[4,24,128]{2,1,0:T(8,128)S(1)} all-to-all(f32[4,24,128]{2,1,0:T(8,128)S(1)} %broadcast_in_dim.18), channel_id=1, replica_groups=mesh['yh'=2,'x'=4,'c'=2,'yl'=4,'zh'=4,'zl'=4] {'zh'}, dimensions={0} | all-to-all | bytes 98304 | tf_op jit(solution)/shard_map/all_to_all | solution.py:187
  150.1 12.8 %all_to_all.42 = f32[16,24,128]{2,1,0:T(8,128)S(1)} all-to-all(f32[16,24,128]{2,1,0:T(8,128)S(1)} %broadcast_in_dim.19), channel_id=1, replica_groups=mesh['yh'=2,'x'=4,'c'=2,'yl'=4,'zh'=4,'zl'=4] {'yl','zl'}, dimensions={0} | all-to-all | bytes 393216 | tf_op jit(solution)/shard_map/all_to_all | solution.py:187
  162.9 10.4 %all_to_all.43.sums_ref = f32[4,352,128]{2,1,0:T(8,128)S(1)} all-to-all(f32[4,352,128]{2,1,0:T(8,128)S(1)} %broadcast_in_dim.40), channel_id=1, replica_groups=mesh['yh'=2,'x'=4,'c'=2,'yl'=4,'zh'=4,'zl'=4] {'x'}, dimensions={0} | all-to-all | bytes 1441792 | tf_op jit(solution)/shard_map/all_to_all | solution.py:187
  173.3 6.7 %collective-permute-start = (f32[4,352,128]{2,1,0:T(8,128)S(1)}, f32[4,352,128]{2,1,0:T(8,128)S(1)}, u32[]{:S(2)}, u32[]{:S(2)}) collective-permute-start(f32[4,352,128]{2,1,0:T(8,128)S(1)} %all_to_all.43.sums_ref), channel_id=1, source_target_pairs={{0,64},{64,0},{1,65},{65,1},{2,66},{66,2},{3,67},{67,3},{4,68},{68... | collective-permute-start | bytes 2162696 | tf_op jit(solution)/shard_map/ppermute | solution.py:303
  180.1 0.1 pad_add_fusion.at_ref
  180.2 1.5 collective-permute-done.sums2_ref
  181.7 25.2 %finish.1 = (f32[64,512]{1,0:T(8,128)}, f32[16,512]{1,0:T(8,128)}) custom-call(s32[2]{0:T(128)S(1)} %pad_add_fusion.at_ref, f32[4,352,128]{2,1,0:T(8,128)S(1)} %all_to_all.43.sums_ref, f32[4,352,128]{2,1,0:T(8,128)S(1)} %collective-permute-done.sums2_ref, f32[256,64]{1,0:T(8,128)S(1)} %get-tuple-element.5.f_ref, f32[64,512]{1,0:T(8,128)S(1)} %copy-done), custom_call_target="tpu_custom_call" | custom-call | tf_op jit(solution)/shard_map/finish/pallas_call | solution.py:167
  (17 shorter events, 0.2 us)
Async XLA Ops:
  0.6 1.5 copy-start.1
  2.1 1.0 copy-start.2
  3.2 0.8 copy-start.3
  4.0 0.7 copy-start.4
  7.0 11.1 %copy-start.5 = (s32[1,2048]{1,0:T(1,128)S(1)}, s32[1,2048]{1,0:T(1,128)}, u32[]{:S(2)}) copy-start(s32[1,2048]{1,0:T(1,128)} %param.10) | copy-start | bytes 24580
  7.0 11.7 %copy-start = (f32[64,512]{1,0:T(8,128)S(1)}, f32[64,512]{1,0:T(8,128)}, u32[]{:S(2)}) copy-start(f32[64,512]{1,0:T(8,128)} %s_ref.1) | copy-start | bytes 393220
  7.0 37.4 %all-to-all-start = ((f32[16,128,128]{2,1,0:T(8,128)}), f32[16,128,128]{2,1,0:T(8,128)S(1)}, u32[]{:S(2)}, u32[]{:S(2)}) async-start(f32[16,128,128]{2,1,0:T(8,128)} %project.1), calls=%async_computation | async-start | bytes 2097152 | tf_op jit(solution)/shard_map/all_to_all | solution.py:187
  45.1 31.0 %all-to-all-start.1 = ((f32[4,32,128]{2,1,0:T(8,128)}), f32[4,32,128]{2,1,0:T(8,128)S(1)}, u32[]{:S(2)}, u32[]{:S(2)}) async-start(f32[4,32,128]{2,1,0:T(8,128)} %bitcast.6), calls=%async_computation.1 | async-start | bytes 131072 | tf_op jit(solution)/shard_map/all_to_all | solution.py:187
  77.6 21.6 %all-to-all-start.2 = ((f32[64,8,128]{2,1,0:T(8,128)}), f32[64,8,128]{2,1,0:T(8,128)S(1)}, u32[]{:S(2)}, u32[]{:S(2)}) async-start(f32[64,8,128]{2,1,0:T(8,128)} %outer.1), calls=%async_computation.2 | async-start | bytes 524288 | tf_op jit(solution)/shard_map/all_to_all | solution.py:187
  100.0 21.6 %all-to-all-start.3 = ((f32[16,8,128]{2,1,0:T(8,128)}), f32[16,8,128]{2,1,0:T(8,128)S(1)}, u32[]{:S(2)}, u32[]{:S(2)}) async-start(f32[16,8,128]{2,1,0:T(8,128)} %broadcast_in_dim.17), calls=%async_computation.3 | async-start | bytes 131072 | tf_op jit(solution)/shard_map/all_to_all | solution.py:187
  173.3 8.4 %collective-permute-start = (f32[4,352,128]{2,1,0:T(8,128)S(1)}, f32[4,352,128]{2,1,0:T(8,128)S(1)}, u32[]{:S(2)}, u32[]{:S(2)}) collective-permute-start(f32[4,352,128]{2,1,0:T(8,128)S(1)} %all_to_all.43.sums_ref), channel_id=1, source_target_pairs={{0,64},{64,0},{1,65},{65,1},{2,66},{66,2},{3,67},{67,3},{4,68},{68... | collective-permute-start | bytes 2162696 | tf_op jit(solution)/shard_map/ppermute | solution.py:303

commit v6 on v5

--- a/solution.py
+++ b/solution.py
@@ -23,13 +23,15 @@
 def factor_block(d_ref, w_ref):
     nb = 128
     full = (8, nb)
+    lane = lax.broadcasted_iota(jnp.int32, full, 1)
     xs = [d_ref[8 * v: 8 * v + 8, :] for v in range(nb // 8)]
-    ws = [w_ref[8 * v: 8 * v + 8, :] for v in range(nb // 8)]
+    diag = [jnp.broadcast_to(xs[0][:, j:j + 1], full) for j in range(8)]
     for p in range(nb // 8):
         base = 8 * p
+        here = (lane >= base) & (lane < base + 8)
         xr = [jnp.broadcast_to(xs[p][i:i + 1, :], full) for i in range(8)]
-        wr = [jnp.broadcast_to(ws[p][i:i + 1, :], full) for i in range(8)]
-        s = [[jnp.broadcast_to(xr[i][:, base + j:base + j + 1], full) for j in range(i + 1)] for i in range(8)]
+        s = [[jnp.broadcast_to(diag[j][i:i + 1, :], full) for j in range(i + 1)] for i in range(8)]
+        xr = [jnp.where(here, jnp.where(lane == base + i, 1.0, 0.0), xr[i]) for i in range(8)]
         m = [[None] * 8 for _ in range(8)]
         inv = [None] * 4
         for k in range(0, 8, 2):
@@ -45,29 +47,50 @@
         for i in range(2, 8):
             for k in range(0, i - i % 2, 2):
                 xr[i] = xr[i] - (m[i][k] * xr[k] + m[i][k + 1] * xr[k + 1])
-                wr[i] = wr[i] - (m[i][k] * wr[k] + m[i][k + 1] * wr[k + 1])
         for k in range(0, 8, 2):
             a, b = s[k][k], s[k + 1][k]
-            w_ref[base + k: base + k + 1, :] = (wr[k] * lax.rsqrt(a))[0:1, :]
             ratio = b / a
-            low = (wr[k + 1] - ratio * wr[k]) * lax.rsqrt(s[k + 1][k + 1] - ratio * b)
-            w_ref[base + k + 1: base + k + 2, :] = low[0:1, :]
+            top = xr[k] * lax.rsqrt(a)
+            low = (xr[k + 1] - ratio * xr[k]) * lax.rsqrt(s[k + 1][k + 1] - ratio * b)
+            w_ref[base + k: base + k + 1, :] = jnp.where(lane < base + 8, top, 0.0)[0:1, :]
+            w_ref[base + k + 1: base + k + 2, :] = jnp.where(lane < base + 8, low, 0.0)[0:1, :]
         if p == nb // 8 - 1:
             break
-        xv, wv = [None] * 8, [None] * 8
+        q = p + 1
+        f = [jnp.broadcast_to(xs[q][:, base + i:base + i + 1], full) for i in range(8)]
+        diag = [jnp.broadcast_to(xs[q][:, base + 8 + j:base + 9 + j], full) for j in range(8)]
+        z = [None] * 8
+        for k in range(0, 8, 2):
+            ia, ib, id_ = inv[k // 2]
+            z[k] = f[k] * ia - f[k + 1] * ib
+            z[k + 1] = f[k + 1] * id_ - f[k] * ib
+            for i in range(k + 2, 8):
+                f[i] = f[i] - (m[i][k] * f[k] + m[i][k + 1] * f[k + 1])
+            for j in range(8):
+                diag[j] = diag[j] - (
+                    z[k] * jnp.broadcast_to(f[k][j:j + 1, :], full)
+                    + z[k + 1] * jnp.broadcast_to(f[k + 1][j:j + 1, :], full)
+                )
+        rest = jnp.where(here, 0.0, xs[q])
+        for k in range(0, 8, 2):
+            rest = rest - (z[k] * xr[k] + z[k + 1] * xr[k + 1])
+        xs[q] = rest
+        xv = [None] * 8
         for k in range(6, -1, -2):
             ia, ib, id_ = inv[k // 2]
-            for rows, out in ((xr, xv), (wr, wv)):
-                out[k] = rows[k] * ia - rows[k + 1] * ib
-                out[k + 1] = rows[k + 1] * id_ - rows[k] * ib
-                for i in range(k + 2, 8):
-                    out[k] = out[k] - m[i][k] * out[i]
-                    out[k + 1] = out[k + 1] - m[i][k + 1] * out[i]
-        for q in range(p + 1, nb // 8):
+            xv[k] = xr[k] * ia - xr[k + 1] * ib
+            xv[k + 1] = xr[k + 1] * id_ - xr[k] * ib
+            for i in range(k + 2, 8):
+                xv[k] = xv[k] - m[i][k] * xv[i]
+                xv[k + 1] = xv[k + 1] - m[i][k + 1] * xv[i]
+        for q in range(p + 2, nb // 8):
             cols = [jnp.broadcast_to(xs[q][:, base + i:base + i + 1], full) for i in range(8)]
-            for i in range(8):
-                xs[q] = xs[q] - cols[i] * xv[i]
-                ws[q] = ws[q] - cols[i] * wv[i]
+            rest = jnp.where(here, 0.0, xs[q])
+            xs[q] = rest - (
+                ((cols[0] * xv[0] + cols[1] * xv[1]) + (cols[2] * xv[2] + cols[3] * xv[3]))
+                + ((cols[4] * xv[4] + cols[5] * xv[5]) + (cols[6] * xv[6] + cols[7] * xv[7]))
+            )
+
 
 def products_kernel(at_ref, tiles_ref, sketch_ref, gram_ref, sums_ref, features_ref):
     groups, half, lanes = tiles_ref.shape
@@ -102,7 +125,7 @@
     )(block, tiles, sketch, gram_rows)
 
 
-def finish_kernel(at_ref, sums_ref, sums2_ref, f_ref, s_ref, ns_ref, co_ref, a_ref, x_ref, k_ref, p_ref, g_ref, d_ref, w_ref):
+def finish_kernel(at_ref, sums_ref, sums2_ref, f_ref, s_ref, ns_ref, co_ref, a_ref, x_ref, k_ref, p_ref, g_ref, d_ref, w_ref, wp_ref):
     n = a_ref.shape[0]
     own, e = f_ref.shape[1], f_ref.shape[0]
     across = sums_ref.shape[0]
@@ -124,36 +147,45 @@
     total_sq = jnp.sum(jnp.sum(jnp.where(er == ec, k, 0.0), axis=0, keepdims=True), axis=1, keepdims=True)
     c = 16.0 / (total_sq + 1e-6)
     q = p + mm(k * c, p, ((1,), (0,)))
+    pq = p + q
+    pc = p * c
+    colid = lax.broadcasted_iota(jnp.int32, (128, n), 1)
+
+    def next_block(o, t):
+        w = w_ref[...]
+        wp_ref[...] = w
+        r = mm(w, a_ref[pl.ds(o, 128), pl.ds(t, 128)], ((1,), (0,)))
+        d_ref[...] = a_ref[pl.ds(t, 128), pl.ds(t, 128)] - mm(r, r, ((0,), (0,)))
+
+    d_ref[...] = g_ref[:128, :] + mm(pc[:, :128], pq[:, :128], ((0,), (0,)))
     x_ref[:own, :] = s_ref[...] + mm(f_ref[...] * c, p, ((0,), (0,)))
     x_ref[own:, :] = q
-    pq = p + q
-    pc = p * c
     at = 0
     for o in range(0, n, 128):
         update = mm(pc[:, o:o + 128], pq[:, o:], ((0,), (0,)))
+        if o > 0:
+            a_ref[o:o + 128, :o] = jnp.zeros((128, o), jnp.float32)
         for to in range(o, n, 128):
             a_ref[o:o + 128, to:to + 128] = g_ref[at:at + 128, :] + update[:, to - o:to - o + 128]
             at += 128
-    ri = lax.broadcasted_iota(jnp.int32, (128, 128), 0)
-    ci = lax.broadcasted_iota(jnp.int32, (128, 128), 1)
+    factor_block(d_ref, w_ref)
+    next_block(0, 128)
 
     def step(b, carry):
         o = pl.multiple_of(b * 128, 128)
-        d_ref[...] = a_ref[pl.ds(o, 128), pl.ds(o, 128)]
-        w_ref[...] = jnp.where(ri == ci, 1.0, 0.0)
+        before = pl.multiple_of(o - 128, 128)
+        wp = wp_ref[...]
+        r = jnp.where(colid >= o, mm(wp, a_ref[pl.ds(before, 128), :], ((1,), (0,))), 0.0)
+        y = mm(x_ref[:, pl.ds(before, 128)], wp, ((1,), (1,)))
+        x_ref[:, pl.ds(before, 128)] = y
+        x_ref[...] = x_ref[...] - mm(y, r, ((1,), (0,)))
+        a_ref[...] = a_ref[...] - mm(r, r, ((0,), (0,)))
         factor_block(d_ref, w_ref)
-        w = w_ref[...]
-        x_ref[:, pl.ds(o, 128)] = mm(x_ref[:, pl.ds(o, 128)], w, ((1,), (1,)))
-        for at in range(0, n - 128, 128):
-            @pl.when(b * 128 == at)
-            def _(at=at):
-                r = mm(w, a_ref[at:at + 128, at + 128:], ((1,), (0,)))
-                x_ref[:, at + 128:] = x_ref[:, at + 128:] - mm(x_ref[:, at:at + 128], r, ((1,), (0,)))
-                for o in range(at + 128, n, 128):
-                    a_ref[o:o + 128, o:] = a_ref[o:o + 128, o:] - mm(r[:, o - at - 128:o - at], r[:, o - at - 128:], ((0,), (0,)))
+        next_block(o, pl.multiple_of(jnp.minimum(o + 128, n - 128), 128))
         return carry
 
-    lax.fori_loop(0, n // 128, step, 0)
+    lax.fori_loop(1, n // 128, step, 0)
+    x_ref[:, n - 128:] = mm(x_ref[:, n - 128:], wp_ref[...], ((1,), (1,)))
     ns_ref[...] = x_ref[:own, :]
     coefs = x_ref[own:, :]
     mean = jnp.sum(coefs * coefs, axis=0, keepdims=True) / e
@@ -177,6 +209,7 @@
             pltpu.VMEM((n * (n + 128) // 256, 128), jnp.float32),
             pltpu.VMEM((128, 128), jnp.float32),
             pltpu.VMEM((128, 128), jnp.float32),
+            pltpu.VMEM((128, 128), jnp.float32),
         ],
         compiler_params=pltpu.CompilerParams(vmem_limit_bytes=40 * 1024 * 1024),
         name="finish",
@@ -214,7 +247,6 @@
             pl.BlockSpec((width, y.shape[1]), lambda i: (0, 0)),
         ],
         out_specs=pl.BlockSpec((step // 128, 2 * width, 128), lambda i: (i, 0, 0)),
-        compiler_params=pltpu.CompilerParams(vmem_limit_bytes=16 * 1024 * 1024),
         name="project",
     )(x, y.T, px.T, py.T)
 

time: 208 us -> 199 us (0.957)
  Pallas kernels: 30.2 us -> 25.6 us
  local copies, waits for them, and re-layouts: 5.43 us -> 1.34 us
    pallas_call x1, Pallas kernels: 25.2 us -> 18.8 us  [finish(): pl.pallas_call(finish_kernel, out_shape=(jax.ShapeDtypeStruct((own, n), j...]
    unnamed x20 -> x12, local copies, waits for them, and re-layouts: 4.18 us -> 0.09 us
where the time goes in v6:
time: 199 us; the launch traced here: 198 us
  waiting for transfers between devices  64.3 us (32%)
  starting transfers between devices  53.6 us (27%)
  blocking collectives  51.3 us (26%)
  Pallas kernels  25.6 us (13%)
    all_to_all x4, waiting for transfers between devices, exchange(): return lax.all_to_all(x, axes, 0, 0, tiled=True)  62.8 us
    all_to_all x4, blocking collectives, exchange(): return lax.all_to_all(x, axes, 0, 0, tiled=True)  51.3 us
    all_to_all x4, starting transfers between devices, exchange(): return lax.all_to_all(x, axes, 0, 0, tiled=True)  46.9 us
    pallas_call x1, Pallas kernels, finish(): pl.pallas_call(finish_kernel, out_shape=(jax.ShapeDtypeStruct((own, n), j...  18.8 us
    ppermute x1, starting transfers between devices, per_device(): other = lax.ppermute(sums, 'c', [(0, 1), (1, 0)])  6.73 us
    pallas_call x1, Pallas kernels, project(): pl.pallas_call(project_kernel, grid=(4,), out_shape=jax.ShapeDtypeStruct(...  4.11 us
  transfers between devices with their start and end apart: 5, of which 5 were waited for; matrix products, arithmetic and copies ran while one was open for 1% of the time, Pallas kernels for 0%

profile of v6, /device:TPU:1, one launch (start us, length us, event | category | flops | bytes accessed | tf_op | source)
XLA Modules:
  0.0 198.3 jit_solution(9814722789618148673)
XLA Ops:
  0.6 4.1 %project.1 = f32[16,128,128]{2,1,0:T(8,128)} custom-call(bf16[2048,128]{1,0:T(8,128)(2,1)} %x_ref.1, bf16[448,2048]{1,0:T(8,128)(2,1)} %bitcast.16, bf16[64,128]{1,0:T(8,128)(2,1)} %bitcast.19, bf16[64,448]{1,0:T(8,128)(2,1)} %bitcast.18), custom_call_target="tpu_custom_call" | custom-call | tf_op jit(solution)/shard_map/project/pallas_call | solution.py:239
  4.7 0.0 copy-start.1
  4.7 0.0 copy-start
  4.7 11.1 %all-to-all-start = ((f32[16,128,128]{2,1,0:T(8,128)}), f32[16,128,128]{2,1,0:T(8,128)S(1)}, u32[]{:S(2)}, u32[]{:S(2)}) async-start(f32[16,128,128]{2,1,0:T(8,128)} %project.1), calls=%async_computation | async-start | bytes 2097152 | tf_op jit(solution)/shard_map/all_to_all | solution.py:220
  15.9 0.0 copy-done.1
  15.9 0.1 dynamic-slice_bitcast_fusion
  15.9 0.1 copy.10.seg_ref
  16.0 0.1 convert_reduce_fusion
  16.2 0.1 reshape.33
  16.2 0.1 copy.11
  16.3 0.1 broadcast_in_dim.16
  16.4 0.1 reshape.34
  16.5 0.0 copy-done
  16.5 1.0 fusion
  17.6 24.5 %all-to-all-done.parts_ref = f32[16,128,128]{2,1,0:T(8,128)S(1)} async-done(((f32[16,128,128]{2,1,0:T(8,128)}), f32[16,128,128]{2,1,0:T(8,128)S(1)}, u32[]{:S(2)}, u32[]{:S(2)}) %all-to-all-start) | async-done | bytes 1048608 | tf_op jit(solution)/shard_map/all_to_all | solution.py:220
  42.1 0.8 fold.1
  42.9 19.3 %all-to-all-start.1 = ((f32[4,32,128]{2,1,0:T(8,128)}), f32[4,32,128]{2,1,0:T(8,128)S(1)}, u32[]{:S(2)}, u32[]{:S(2)}) async-start(f32[4,32,128]{2,1,0:T(8,128)} %bitcast.6), calls=%async_computation.1 | async-start | bytes 131072 | tf_op jit(solution)/shard_map/all_to_all | solution.py:220
  62.1 11.7 %all-to-all-done.1.part_ref = f32[4,32,128]{2,1,0:T(8,128)S(1)} async-done(((f32[4,32,128]{2,1,0:T(8,128)}), f32[4,32,128]{2,1,0:T(8,128)S(1)}, u32[]{:S(2)}, u32[]{:S(2)}) %all-to-all-start.1) | async-done | bytes 65568 | tf_op jit(solution)/shard_map/all_to_all | solution.py:220
  73.8 1.6 outer.1
  75.4 4.6 %all-to-all-start.2 = ((f32[64,8,128]{2,1,0:T(8,128)}), f32[64,8,128]{2,1,0:T(8,128)S(1)}, u32[]{:S(2)}, u32[]{:S(2)}) async-start(f32[64,8,128]{2,1,0:T(8,128)} %outer.1), calls=%async_computation.2 | async-start | bytes 524288 | tf_op jit(solution)/shard_map/all_to_all | solution.py:220
  80.1 16.9 %all-to-all-done.2 = f32[64,8,128]{2,1,0:T(8,128)S(1)} async-done(((f32[64,8,128]{2,1,0:T(8,128)}), f32[64,8,128]{2,1,0:T(8,128)S(1)}, u32[]{:S(2)}, u32[]{:S(2)}) %all-to-all-start.2) | async-done | bytes 262176 | tf_op jit(solution)/shard_map/all_to_all | solution.py:220
  97.0 0.1 reduce_sum.36
  97.0 0.6 broadcast_in_dim.17
  97.7 11.9 %all-to-all-start.3 = ((f32[16,8,128]{2,1,0:T(8,128)}), f32[16,8,128]{2,1,0:T(8,128)S(1)}, u32[]{:S(2)}, u32[]{:S(2)}) async-start(f32[16,8,128]{2,1,0:T(8,128)} %broadcast_in_dim.17), calls=%async_computation.3 | async-start | bytes 131072 | tf_op jit(solution)/shard_map/all_to_all | solution.py:220
  109.6 9.7 %all-to-all-done.3.tiles_ref = f32[16,8,128]{2,1,0:T(8,128)S(1)} async-done(((f32[16,8,128]{2,1,0:T(8,128)}), f32[16,8,128]{2,1,0:T(8,128)S(1)}, u32[]{:S(2)}, u32[]{:S(2)}) %all-to-all-start.3) | async-done | bytes 65568 | tf_op jit(solution)/shard_map/all_to_all | solution.py:220
  119.3 0.4 products.1
  119.7 12.8 %all_to_all.40 = f32[16,24,128]{2,1,0:T(8,128)S(1)} all-to-all(f32[16,24,128]{2,1,0:T(8,128)S(1)} %bitcast.15), channel_id=1, replica_groups=mesh['yh'=2,'x'=4,'c'=2,'yl'=4,'zh'=4,'zl'=4] {'yl','zl'}, dimensions={0} | all-to-all | bytes 393216 | tf_op jit(solution)/shard_map/all_to_all | solution.py:220
  132.5 15.3 %all_to_all.41 = f32[4,24,128]{2,1,0:T(8,128)S(1)} all-to-all(f32[4,24,128]{2,1,0:T(8,128)S(1)} %broadcast_in_dim.18), channel_id=1, replica_groups=mesh['yh'=2,'x'=4,'c'=2,'yl'=4,'zh'=4,'zl'=4] {'zh'}, dimensions={0} | all-to-all | bytes 98304 | tf_op jit(solution)/shard_map/all_to_all | solution.py:220
  147.8 12.8 %all_to_all.42 = f32[16,24,128]{2,1,0:T(8,128)S(1)} all-to-all(f32[16,24,128]{2,1,0:T(8,128)S(1)} %broadcast_in_dim.19), channel_id=1, replica_groups=mesh['yh'=2,'x'=4,'c'=2,'yl'=4,'zh'=4,'zl'=4] {'yl','zl'}, dimensions={0} | all-to-all | bytes 393216 | tf_op jit(solution)/shard_map/all_to_all | solution.py:220
  160.7 10.4 %all_to_all.43.sums_ref = f32[4,352,128]{2,1,0:T(8,128)S(1)} all-to-all(f32[4,352,128]{2,1,0:T(8,128)S(1)} %broadcast_in_dim.40), channel_id=1, replica_groups=mesh['yh'=2,'x'=4,'c'=2,'yl'=4,'zh'=4,'zl'=4] {'x'}, dimensions={0} | all-to-all | bytes 1441792 | tf_op jit(solution)/shard_map/all_to_all | solution.py:220
  171.1 6.7 %collective-permute-start = (f32[4,352,128]{2,1,0:T(8,128)S(1)}, f32[4,352,128]{2,1,0:T(8,128)S(1)}, u32[]{:S(2)}, u32[]{:S(2)}) collective-permute-start(f32[4,352,128]{2,1,0:T(8,128)S(1)} %all_to_all.43.sums_ref), channel_id=1, source_target_pairs={{0,64},{64,0},{1,65},{65,1},{2,66},{66,2},{3,67},{67,3},{4,68},{68... | collective-permute-start | bytes 2162696 | tf_op jit(solution)/shard_map/ppermute | solution.py:335
  177.8 0.1 pad_add_fusion.at_ref
  177.9 1.5 collective-permute-done.sums2_ref
  179.4 18.8 %finish.1 = (f32[64,512]{1,0:T(8,128)}, f32[16,512]{1,0:T(8,128)}) custom-call(s32[2]{0:T(128)S(1)} %pad_add_fusion.at_ref, f32[4,352,128]{2,1,0:T(8,128)S(1)} %all_to_all.43.sums_ref, f32[4,352,128]{2,1,0:T(8,128)S(1)} %collective-permute-done.sums2_ref, f32[256,64]{1,0:T(8,128)S(1)} %get-tuple-element.5.f_ref, f32[64,512]{1,0:T(8,128)S(1)} %copy-done), custom_call_target="tpu_custom_call" | custom-call | tf_op jit(solution)/shard_map/finish/pallas_call | solution.py:199
  (17 shorter events, 0.2 us)
Async XLA Ops:
  4.7 11.1 %copy-start.1 = (s32[1,2048]{1,0:T(1,128)S(1)}, s32[1,2048]{1,0:T(1,128)}, u32[]{:S(2)}) copy-start(s32[1,2048]{1,0:T(1,128)} %param.10) | copy-start | bytes 24580
  4.7 11.8 %copy-start = (f32[64,512]{1,0:T(8,128)S(1)}, f32[64,512]{1,0:T(8,128)}, u32[]{:S(2)}) copy-start(f32[64,512]{1,0:T(8,128)} %s_ref.1) | copy-start | bytes 393220
  4.7 37.4 %all-to-all-start = ((f32[16,128,128]{2,1,0:T(8,128)}), f32[16,128,128]{2,1,0:T(8,128)S(1)}, u32[]{:S(2)}, u32[]{:S(2)}) async-start(f32[16,128,128]{2,1,0:T(8,128)} %project.1), calls=%async_computation | async-start | bytes 2097152 | tf_op jit(solution)/shard_map/all_to_all | solution.py:220
  42.9 31.0 %all-to-all-start.1 = ((f32[4,32,128]{2,1,0:T(8,128)}), f32[4,32,128]{2,1,0:T(8,128)S(1)}, u32[]{:S(2)}, u32[]{:S(2)}) async-start(f32[4,32,128]{2,1,0:T(8,128)} %bitcast.6), calls=%async_computation.1 | async-start | bytes 131072 | tf_op jit(solution)/shard_map/all_to_all | solution.py:220
  75.4 21.6 %all-to-all-start.2 = ((f32[64,8,128]{2,1,0:T(8,128)}), f32[64,8,128]{2,1,0:T(8,128)S(1)}, u32[]{:S(2)}, u32[]{:S(2)}) async-start(f32[64,8,128]{2,1,0:T(8,128)} %outer.1), calls=%async_computation.2 | async-start | bytes 524288 | tf_op jit(solution)/shard_map/all_to_all | solution.py:220
  97.7 21.6 %all-to-all-start.3 = ((f32[16,8,128]{2,1,0:T(8,128)}), f32[16,8,128]{2,1,0:T(8,128)S(1)}, u32[]{:S(2)}, u32[]{:S(2)}) async-start(f32[16,8,128]{2,1,0:T(8,128)} %broadcast_in_dim.17), calls=%async_computation.3 | async-start | bytes 131072 | tf_op jit(solution)/shard_map/all_to_all | solution.py:220
  171.1 8.4 %collective-permute-start = (f32[4,352,128]{2,1,0:T(8,128)S(1)}, f32[4,352,128]{2,1,0:T(8,128)S(1)}, u32[]{:S(2)}, u32[]{:S(2)}) collective-permute-start(f32[4,352,128]{2,1,0:T(8,128)S(1)} %all_to_all.43.sums_ref), channel_id=1, source_target_pairs={{0,64},{64,0},{1,65},{65,1},{2,66},{66,2},{3,67},{67,3},{4,68},{68... | collective-permute-start | bytes 2162696 | tf_op jit(solution)/shard_map/ppermute | solution.py:335

commit v7 on v6

--- a/solution.py
+++ b/solution.py
@@ -235,10 +235,10 @@
 
 def project(x, y, px, py):
     tokens, width = x.shape[0], px.shape[1]
-    step = tokens // 4
+    step = tokens // 2
     return pl.pallas_call(
         project_kernel,
-        grid=(4,),
+        grid=(2,),
         out_shape=jax.ShapeDtypeStruct((tokens // 128, 2 * width, 128), jnp.float32),
         in_specs=[
             pl.BlockSpec((step, x.shape[1]), lambda i: (i, 0)),

time: 199 us -> 198 us (level)
  no operation moved by 1% of the time
where the time goes in v7:
time: 198 us; the launch traced here: 197 us
  waiting for transfers between devices  64.2 us (32%)
  starting transfers between devices  53.7 us (27%)
  blocking collectives  51.3 us (26%)
  Pallas kernels  24.4 us (12%)
    all_to_all x4, waiting for transfers between devices, exchange(): return lax.all_to_all(x, axes, 0, 0, tiled=True)  62.7 us
    all_to_all x4, blocking collectives, exchange(): return lax.all_to_all(x, axes, 0, 0, tiled=True)  51.3 us
    all_to_all x4, starting transfers between devices, exchange(): return lax.all_to_all(x, axes, 0, 0, tiled=True)  47 us
    pallas_call x1, Pallas kernels, finish(): pl.pallas_call(finish_kernel, out_shape=(jax.ShapeDtypeStruct((own, n), j...  18.8 us
    ppermute x1, starting transfers between devices, per_device(): other = lax.ppermute(sums, 'c', [(0, 1), (1, 0)])  6.73 us
  transfers between devices with their start and end apart: 5, of which 5 were waited for; matrix products, arithmetic and copies ran while one was open for 1% of the time, Pallas kernels for 0%

profile of v7, /device:TPU:1, one launch (start us, length us, event | category | flops | bytes accessed | tf_op | source)
XLA Modules:
  0.0 197.0 jit_solution(14485055028877002492)
XLA Ops:
  0.6 2.9 %project.1 = f32[16,128,128]{2,1,0:T(8,128)} custom-call(bf16[2048,128]{1,0:T(8,128)(2,1)} %x_ref.1, bf16[448,2048]{1,0:T(8,128)(2,1)} %bitcast.16, bf16[64,128]{1,0:T(8,128)(2,1)} %bitcast.19, bf16[64,448]{1,0:T(8,128)(2,1)} %bitcast.18), custom_call_target="tpu_custom_call" | custom-call | tf_op jit(solution)/shard_map/project/pallas_call | solution.py:239
  3.5 0.0 copy-start.1
  3.5 0.0 copy-start
  3.5 11.1 %all-to-all-start = ((f32[16,128,128]{2,1,0:T(8,128)}), f32[16,128,128]{2,1,0:T(8,128)S(1)}, u32[]{:S(2)}, u32[]{:S(2)}) async-start(f32[16,128,128]{2,1,0:T(8,128)} %project.1), calls=%async_computation | async-start | bytes 2097152 | tf_op jit(solution)/shard_map/all_to_all | solution.py:220
  14.6 0.0 copy-done.1
  14.6 0.1 dynamic-slice_bitcast_fusion
  14.7 0.1 copy.10.seg_ref
  14.8 0.1 convert_reduce_fusion
  14.9 0.1 reshape.33
  15.0 0.1 copy.11
  15.1 0.1 broadcast_in_dim.16
  15.2 0.1 reshape.34
  15.2 0.0 copy-done
  15.3 1.0 fusion
  16.3 24.5 %all-to-all-done.parts_ref = f32[16,128,128]{2,1,0:T(8,128)S(1)} async-done(((f32[16,128,128]{2,1,0:T(8,128)}), f32[16,128,128]{2,1,0:T(8,128)S(1)}, u32[]{:S(2)}, u32[]{:S(2)}) %all-to-all-start) | async-done | bytes 1048608 | tf_op jit(solution)/shard_map/all_to_all | solution.py:220
  40.9 0.8 fold.1
  41.6 19.3 %all-to-all-start.1 = ((f32[4,32,128]{2,1,0:T(8,128)}), f32[4,32,128]{2,1,0:T(8,128)S(1)}, u32[]{:S(2)}, u32[]{:S(2)}) async-start(f32[4,32,128]{2,1,0:T(8,128)} %bitcast.6), calls=%async_computation.1 | async-start | bytes 131072 | tf_op jit(solution)/shard_map/all_to_all | solution.py:220
  60.9 11.7 %all-to-all-done.1.part_ref = f32[4,32,128]{2,1,0:T(8,128)S(1)} async-done(((f32[4,32,128]{2,1,0:T(8,128)}), f32[4,32,128]{2,1,0:T(8,128)S(1)}, u32[]{:S(2)}, u32[]{:S(2)}) %all-to-all-start.1) | async-done | bytes 65568 | tf_op jit(solution)/shard_map/all_to_all | solution.py:220
  72.6 1.6 outer.1
  74.1 4.6 %all-to-all-start.2 = ((f32[64,8,128]{2,1,0:T(8,128)}), f32[64,8,128]{2,1,0:T(8,128)S(1)}, u32[]{:S(2)}, u32[]{:S(2)}) async-start(f32[64,8,128]{2,1,0:T(8,128)} %outer.1), calls=%async_computation.2 | async-start | bytes 524288 | tf_op jit(solution)/shard_map/all_to_all | solution.py:220
  78.8 16.8 %all-to-all-done.2 = f32[64,8,128]{2,1,0:T(8,128)S(1)} async-done(((f32[64,8,128]{2,1,0:T(8,128)}), f32[64,8,128]{2,1,0:T(8,128)S(1)}, u32[]{:S(2)}, u32[]{:S(2)}) %all-to-all-start.2) | async-done | bytes 262176 | tf_op jit(solution)/shard_map/all_to_all | solution.py:220
  95.6 0.1 reduce_sum.36
  95.7 0.6 broadcast_in_dim.17
  96.3 12.0 %all-to-all-start.3 = ((f32[16,8,128]{2,1,0:T(8,128)}), f32[16,8,128]{2,1,0:T(8,128)S(1)}, u32[]{:S(2)}, u32[]{:S(2)}) async-start(f32[16,8,128]{2,1,0:T(8,128)} %broadcast_in_dim.17), calls=%async_computation.3 | async-start | bytes 131072 | tf_op jit(solution)/shard_map/all_to_all | solution.py:220
  108.4 9.7 %all-to-all-done.3.tiles_ref = f32[16,8,128]{2,1,0:T(8,128)S(1)} async-done(((f32[16,8,128]{2,1,0:T(8,128)}), f32[16,8,128]{2,1,0:T(8,128)S(1)}, u32[]{:S(2)}, u32[]{:S(2)}) %all-to-all-start.3) | async-done | bytes 65568 | tf_op jit(solution)/shard_map/all_to_all | solution.py:220
  118.1 0.4 products.1
  118.4 12.8 %all_to_all.40 = f32[16,24,128]{2,1,0:T(8,128)S(1)} all-to-all(f32[16,24,128]{2,1,0:T(8,128)S(1)} %bitcast.15), channel_id=1, replica_groups=mesh['yh'=2,'x'=4,'c'=2,'yl'=4,'zh'=4,'zl'=4] {'yl','zl'}, dimensions={0} | all-to-all | bytes 393216 | tf_op jit(solution)/shard_map/all_to_all | solution.py:220
  131.3 15.3 %all_to_all.41 = f32[4,24,128]{2,1,0:T(8,128)S(1)} all-to-all(f32[4,24,128]{2,1,0:T(8,128)S(1)} %broadcast_in_dim.18), channel_id=1, replica_groups=mesh['yh'=2,'x'=4,'c'=2,'yl'=4,'zh'=4,'zl'=4] {'zh'}, dimensions={0} | all-to-all | bytes 98304 | tf_op jit(solution)/shard_map/all_to_all | solution.py:220
  146.6 12.8 %all_to_all.42 = f32[16,24,128]{2,1,0:T(8,128)S(1)} all-to-all(f32[16,24,128]{2,1,0:T(8,128)S(1)} %broadcast_in_dim.19), channel_id=1, replica_groups=mesh['yh'=2,'x'=4,'c'=2,'yl'=4,'zh'=4,'zl'=4] {'yl','zl'}, dimensions={0} | all-to-all | bytes 393216 | tf_op jit(solution)/shard_map/all_to_all | solution.py:220
  159.4 10.4 %all_to_all.43.sums_ref = f32[4,352,128]{2,1,0:T(8,128)S(1)} all-to-all(f32[4,352,128]{2,1,0:T(8,128)S(1)} %broadcast_in_dim.40), channel_id=1, replica_groups=mesh['yh'=2,'x'=4,'c'=2,'yl'=4,'zh'=4,'zl'=4] {'x'}, dimensions={0} | all-to-all | bytes 1441792 | tf_op jit(solution)/shard_map/all_to_all | solution.py:220
  169.8 6.7 %collective-permute-start = (f32[4,352,128]{2,1,0:T(8,128)S(1)}, f32[4,352,128]{2,1,0:T(8,128)S(1)}, u32[]{:S(2)}, u32[]{:S(2)}) collective-permute-start(f32[4,352,128]{2,1,0:T(8,128)S(1)} %all_to_all.43.sums_ref), channel_id=1, source_target_pairs={{0,64},{64,0},{1,65},{65,1},{2,66},{66,2},{3,67},{67,3},{4,68},{68... | collective-permute-start | bytes 2162696 | tf_op jit(solution)/shard_map/ppermute | solution.py:335
  176.6 0.1 pad_add_fusion.at_ref
  176.7 1.5 collective-permute-done.sums2_ref
  178.2 18.8 %finish.1 = (f32[64,512]{1,0:T(8,128)}, f32[16,512]{1,0:T(8,128)}) custom-call(s32[2]{0:T(128)S(1)} %pad_add_fusion.at_ref, f32[4,352,128]{2,1,0:T(8,128)S(1)} %all_to_all.43.sums_ref, f32[4,352,128]{2,1,0:T(8,128)S(1)} %collective-permute-done.sums2_ref, f32[256,64]{1,0:T(8,128)S(1)} %get-tuple-element.5.f_ref, f32[64,512]{1,0:T(8,128)S(1)} %copy-done), custom_call_target="tpu_custom_call" | custom-call | tf_op jit(solution)/shard_map/finish/pallas_call | solution.py:199
  (17 shorter events, 0.2 us)
Async XLA Ops:
  3.5 11.1 %copy-start.1 = (s32[1,2048]{1,0:T(1,128)S(1)}, s32[1,2048]{1,0:T(1,128)}, u32[]{:S(2)}) copy-start(s32[1,2048]{1,0:T(1,128)} %param.10) | copy-start | bytes 24580
  3.5 11.8 %copy-start = (f32[64,512]{1,0:T(8,128)S(1)}, f32[64,512]{1,0:T(8,128)}, u32[]{:S(2)}) copy-start(f32[64,512]{1,0:T(8,128)} %s_ref.1) | copy-start | bytes 393220
  3.5 37.4 %all-to-all-start = ((f32[16,128,128]{2,1,0:T(8,128)}), f32[16,128,128]{2,1,0:T(8,128)S(1)}, u32[]{:S(2)}, u32[]{:S(2)}) async-start(f32[16,128,128]{2,1,0:T(8,128)} %project.1), calls=%async_computation | async-start | bytes 2097152 | tf_op jit(solution)/shard_map/all_to_all | solution.py:220
  41.6 31.0 %all-to-all-start.1 = ((f32[4,32,128]{2,1,0:T(8,128)}), f32[4,32,128]{2,1,0:T(8,128)S(1)}, u32[]{:S(2)}, u32[]{:S(2)}) async-start(f32[4,32,128]{2,1,0:T(8,128)} %bitcast.6), calls=%async_computation.1 | async-start | bytes 131072 | tf_op jit(solution)/shard_map/all_to_all | solution.py:220
  74.1 21.5 %all-to-all-start.2 = ((f32[64,8,128]{2,1,0:T(8,128)}), f32[64,8,128]{2,1,0:T(8,128)S(1)}, u32[]{:S(2)}, u32[]{:S(2)}) async-start(f32[64,8,128]{2,1,0:T(8,128)} %outer.1), calls=%async_computation.2 | async-start | bytes 524288 | tf_op jit(solution)/shard_map/all_to_all | solution.py:220
  96.3 21.7 %all-to-all-start.3 = ((f32[16,8,128]{2,1,0:T(8,128)}), f32[16,8,128]{2,1,0:T(8,128)S(1)}, u32[]{:S(2)}, u32[]{:S(2)}) async-start(f32[16,8,128]{2,1,0:T(8,128)} %broadcast_in_dim.17), calls=%async_computation.3 | async-start | bytes 131072 | tf_op jit(solution)/shard_map/all_to_all | solution.py:220
  169.8 8.4 %collective-permute-start = (f32[4,352,128]{2,1,0:T(8,128)S(1)}, f32[4,352,128]{2,1,0:T(8,128)S(1)}, u32[]{:S(2)}, u32[]{:S(2)}) collective-permute-start(f32[4,352,128]{2,1,0:T(8,128)S(1)} %all_to_all.43.sums_ref), channel_id=1, source_target_pairs={{0,64},{64,0},{1,65},{65,1},{2,66},{66,2},{3,67},{67,3},{4,68},{68... | collective-permute-start | bytes 2162696 | tf_op jit(solution)/shard_map/ppermute | solution.py:335
